TPU v7x, 32 devices: a whole 2x2x4 slice. The times are simulated.
32 devices in a mesh: grp: 2 (over y), tm: 4 (over z), spin: 2 (over core), rows: 2 (over x).
Axes of the slice: x: 2, y: 2, z: 4, core: 2. Of those that a mesh axis runs over, the one named last changes fastest.
Arguments:
- ising_field: int32 [32, 768], P(('grp', 'tm')), parts along dimension 0, may hold values from 0 to 1
- bond_sites: int32 [3072, 2], replicated, may hold values from 0 to 767
- hopping: float32 [3072], replicated, may hold values from 0.5 to 2
- tile_cols: int32 [6, 3], replicated, may hold values from 0 to 5, as said below
Outputs:
- xcorr: float32 [2, 8, 768, 768], P('spin', ('grp', 'tm'), None, 'rows'), parts along dimension 1
There are 2 independent parts, one for each index of `grp`. A program takes and returns all parts, laid end to end along the dimension named above; an argument that names none is the same for every part. Nothing has to cross between parts.
Inputs may be any that keep to these rules, and one draw needn't show every extreme that they name: `ising_field`: 0 stands for the field value -1 and 1 for +1. `bond_sites`: A bond whose tile pair is not in tile_cols adds nothing to H, because tile_mask removes it; its entry in `hopping` is not zero. `tile_cols`: row r lists r first and then the two tiles beside r on a cycle through all 6 tiles drawn from the seed, so each tile row names 3 distinct tiles and the pattern is symmetric.
All inputs are finite; a program needn't handle non-finite values.
Results may differ from a plain program's by a relative error of at most 0.0003.
Values sent between devices are 32-bit elements; how exact they have to be, the bound alone decides.
No kernel may reach another device: no remote copies, remote signals or barrier semaphores. Data moves between devices by JAX's collectives and lax.ppermute only.
A program may use at most 64 MiB of HBM per device.

v0:
```python
import math

import jax
import jax.numpy as jnp
from jax import lax
from jax.sharding import PartitionSpec as P

series_terms = 4


def from_behind(x, axis, by):
    size = lax.axis_size(axis)
    return lax.ppermute(x, axis, [(i, (i + by) % size) for i in range(size)])


def partner_2(value, axis, bit):
    mask = 2**bit
    pairs = [(source, source ^ mask) for source in range(lax.axis_size(axis))]
    return lax.ppermute(value, axis, pairs)


def matmul_hi(left, right):
    return jnp.dot(left, right, precision=lax.Precision.HIGHEST, preferred_element_type=jnp.float32)


def build_kinetic(bond_sites, hopping, tile_cols, matrix_order, hop_scale):
    n_tiles = tile_cols.shape[0]
    tile_len = matrix_order // n_tiles
    tile_mask = jnp.any(
        tile_cols[:, :, None] == jnp.arange(n_tiles, dtype=jnp.int32)[None, None, :], axis=1
    ).astype(jnp.float32)
    site_from = bond_sites[:, 0]
    site_to = bond_sites[:, 1]
    kept_mask = tile_mask[site_from // tile_len, site_to // tile_len]
    weights = hopping * kept_mask
    hop_matrix = jnp.zeros((matrix_order, matrix_order), jnp.float32)
    hop_matrix = hop_matrix.at[site_from, site_to].add(weights).at[site_to, site_from].add(weights)
    return jnp.eye(matrix_order, dtype=jnp.float32) + hop_scale * hop_matrix


def fold_product(current, piece):
    return matmul_hi(piece, current)


def fold_series(power, green, square_it, apply_it):

    def accumulate(totals, piece, start):
        power_total, green_total = totals
        if square_it:
            power_total = matmul_hi(piece, power)
        if apply_it:
            green_total = matmul_hi(piece, green)
        return (power_total, green_total)

    return accumulate


def per_device(ising_field, bond_sites, hopping, tile_cols):
    slices_here, matrix_order = ising_field.shape
    n_tiles, tile_count = tile_cols.shape
    tile_len = matrix_order // n_tiles
    col_width = matrix_order // lax.axis_size("rows")
    n_time = lax.axis_size("tm")
    total_slices = slices_here * n_time
    coupling = 1.5 / math.sqrt(total_slices)
    kinetic = build_kinetic(bond_sites, hopping, tile_cols, matrix_order, 0.5 / total_slices)
    spin_sign = 1.0 - 2.0 * lax.axis_index("spin").astype(jnp.float32)
    spins_pm = (2 * ising_field - 1).astype(jnp.float32)
    factors = jnp.exp(spin_sign * coupling * spins_pm)
    offset = lax.axis_index("rows") * col_width
    tiled = kinetic.reshape(n_tiles, tile_len, n_tiles, tile_len).transpose(0, 2, 1, 3)
    k_tiles = tiled[jnp.arange(n_tiles, dtype=jnp.int32)[:, None], tile_cols]
    cluster = factors[0][:, None] * lax.dynamic_slice_in_dim(kinetic, offset, col_width, 1)

    def slice_step(slice_pos, current):
        gathered = current.reshape(n_tiles, tile_len, col_width)[tile_cols]
        product = jnp.einsum(
            "rjab,rjbc->rac",
            k_tiles,
            gathered,
            precision=lax.Precision.HIGHEST,
            preferred_element_type=jnp.float32,
        )
        return factors[slice_pos][:, None] * product.reshape(matrix_order, col_width)

    cluster = lax.fori_loop(1, slices_here, slice_step, cluster)
    time_steps = n_time.bit_length() - 1
    propagator = cluster
    for level in range(time_steps):
        distant = from_behind(propagator, "tm", -(1 << level))
        empty = jnp.zeros((matrix_order, col_width), jnp.float32)
        propagator = fold_product(propagator, lax.all_gather(distant, "rows", axis=1, tiled=True))
    col_max = lax.pmax(jnp.max(jnp.sum(propagator, axis=0)), "rows")
    power = propagator / (2.0 * col_max)
    row_ids = jnp.arange(matrix_order, dtype=jnp.int32)[:, None]
    col_ids = offset + jnp.arange(col_width, dtype=jnp.int32)[None, :]
    eye_cols = (row_ids == col_ids).astype(jnp.float32)
    green = eye_cols - power
    for level in range(series_terms):
        square_it = level + 1 < series_terms
        apply_it = level > 0
        empty = jnp.zeros((matrix_order, col_width), jnp.float32)
        folder = fold_series(power, green, square_it, apply_it)
        next_power, green_term = folder(
            (empty, empty), lax.all_gather(power, "rows", axis=1, tiled=True), jnp.int32(0)
        )
        if apply_it:
            green = green + green_term
        if square_it:
            power = next_power
    partner = partner_2(green, "spin", 0)
    rows_block = lax.all_to_all(partner, "rows", split_axis=0, concat_axis=1, tiled=True)
    other_trans = rows_block.T
    xcorr = green * (eye_cols - other_trans)
    return xcorr[None, None]


def solution(mesh):
    placed = (P(("grp", "tm"), None), P(), P(), P())
    return jax.shard_map(
        per_device,
        mesh=mesh,
        in_specs=placed,
        out_specs=P("spin", ("grp", "tm"), None, "rows"),
        check_vma=False,
    )
```

profile of v0, /device:TPU:0, one launch (start us, length us, event | category | flops | bytes accessed | tf_op | source)
XLA Modules:
  0.0 485.4 jit_solution(5524657605917395206)
XLA Ops:
  6.5 0.8 fusion.10
  7.3 0.7 fusion.14
  8.0 1.0 fusion.7
  9.0 0.1 and_reduce_fusion
  9.1 0.8 multiply_reduce_fusion
  9.9 13.4 %gather_fusion.1 = f32[3072]{0:T(1024)S(1)} fusion(f32[6,6]{1,0:T(8,128)S(1)} %convert_element_type.19, s32[3072]{0:T(1024)S(1)} %bitcast.64), kind=kCustom, calls=%fused_computation.1 | custom fusion | bytes 49152 | tf_op jit(solution)/shard_map/gather | solution.py:34
  23.4 17.1 %scatter_custom_fusion = f32[589824]{0:T(1024)S(1)} fusion(s32[3072]{0:T(1024)S(1)} %get-tuple-element.158, f32[3072]{0:T(1024)S(1)} %mul.88, f32[]{:T(128)} %constant.99.clone.1), kind=kCustom, calls=%fused_computation.20 | custom fusion | flops 3072 | bytes 2359300
  40.6 17.8 %scatter_fusion = f32[589824]{0:T(1024)S(1)} fusion(f32[589824]{0:T(1024)S(1)} %scatter_custom_fusion, s32[3072]{0:T(1024)S(1)} %get-tuple-element.157, f32[3072]{0:T(1024)S(1)} %mul.88), kind=kCustom, calls=%fused_computation.4 | custom fusion | flops 3072 | bytes 49152
  58.4 1.6 broadcast_multiply_fusion
  59.9 3.4 reshape.67
  63.3 1.8 convert_add_fusion
  65.2 0.6 copy-done.8
  65.8 1.9 reshape.56
  67.6 3.7 copy.20
  71.6 0.2 dynamic-slice_multiply_fusion
  71.7 3.4 gather_fusion.2
  75.1 31.4 %while.15 = (s32[]{:T(128)}, f32[768,384]{1,0:T(8,128)S(1)}, f32[4,768]{1,0:T(4,128)}, s32[6,3]{0,1:T(4,128)S(1)}, f32[6,3,128,128]{3,2,1,0:T(8,128)}, /*index=5*/s32[]{:T(128)}, s32[]{:T(128)}, s32[]{:T(128)}) while((s32[]{:T(128)}, f32[768,384]{1,0:T(8,128)S(1)}, f32[4,768]{1,0:T(4,128)}, s32[6,3]{0,1:T(4,128)S(1)}, ...), condition=%wide.region_4.5_spmd, body=%wide.region_3.4_spmd.sunk | while | flops 1359250432 | bytes 20068060 | solution.py:86
  75.1 0.1 copy.22
  75.3 0.8 copy-done
  76.2 2.0 gather_fusion
  78.2 5.2 %fusion.43 = f32[6,384,128,1]{1,2,3,0:T(8,128)} fusion(f32[6,3,128,384]{3,2,1,0:T(8,128)S(1)} %bitcast.62, f32[6,3,128,128]{3,2,1,0:T(8,128)} %get-tuple-element.210), kind=kOutput, calls=%fused_computation.62.clone.1 | convolution fusion | flops 1358954496 | bytes 5898240 | tf_op jit(solution)/shard_map/while/body/eval_jaxpr/rjab,rjbc->rac/dot_general | solution.py:77
  83.4 0.7 dynamic-slice_reduce_fusion.2
  84.2 1.4 bitcast_multiply_fusion.2
  85.6 0.1 copy.22
  85.8 0.8 copy-done
  86.6 2.0 gather_fusion
  88.7 5.2 %fusion.43 = f32[6,384,128,1]{1,2,3,0:T(8,128)} fusion(f32[6,3,128,384]{3,2,1,0:T(8,128)S(1)} %bitcast.62, f32[6,3,128,128]{3,2,1,0:T(8,128)} %get-tuple-element.210), kind=kOutput, calls=%fused_computation.62.clone.1 | convolution fusion | flops 1358954496 | bytes 5898240 | tf_op jit(solution)/shard_map/while/body/eval_jaxpr/rjab,rjbc->rac/dot_general | solution.py:77
  93.9 0.7 dynamic-slice_reduce_fusion.2
  94.6 1.4 bitcast_multiply_fusion.2
  96.1 0.1 copy.22
  96.3 0.8 copy-done
  97.1 2.0 gather_fusion
  99.2 5.2 %fusion.43 = f32[6,384,128,1]{1,2,3,0:T(8,128)} fusion(f32[6,3,128,384]{3,2,1,0:T(8,128)S(1)} %bitcast.62, f32[6,3,128,128]{3,2,1,0:T(8,128)} %get-tuple-element.210), kind=kOutput, calls=%fused_computation.62.clone.1 | convolution fusion | flops 1358954496 | bytes 5898240 | tf_op jit(solution)/shard_map/while/body/eval_jaxpr/rjab,rjbc->rac/dot_general | solution.py:77
  104.4 0.7 dynamic-slice_reduce_fusion.2
  105.1 1.4 bitcast_multiply_fusion.2
  106.6 5.1 %collective-permute-start = (f32[768,384]{1,0:T(8,128)S(1)}, f32[768,384]{1,0:T(8,128)S(1)}, u32[]{:S(2)}, u32[]{:S(2)}) collective-permute-start(f32[768,384]{1,0:T(8,128)S(1)} %get-tuple-element.137), channel_id=1, source_target_pairs={{0,12},{4,0},{8,4},{12,8},{1,13},{5,1},{9,5},{13,9},{2,14},{6,2},{... | collective-permute-start | bytes 3538952 | tf_op jit(solution)/shard_map/ppermute | solution.py:13
  111.7 25.2 %collective-permute-done = f32[768,384]{1,0:T(8,128)S(1)} collective-permute-done((f32[768,384]{1,0:T(8,128)S(1)}, f32[768,384]{1,0:T(8,128)S(1)}, u32[]{:S(2)}, u32[]{:S(2)}) %collective-permute-start) | collective-permute-done | bytes 1179680 | tf_op jit(solution)/shard_map/ppermute | solution.py:13
  136.9 1.0 copy-done.5
  138.0 0.2 all-gather.9.cloned.1.call-start
  138.2 37.9 %all-gather.7.cloned.1.call-done = f32[768,768]{1,0:T(8,128)} async-done(((f32[768,384]{1,0:T(8,128)}), f32[768,768]{1,0:T(8,128)}) %all-gather.7.cloned.1.call-update) | async-done | bytes 2359312 | tf_op jit(solution)/shard_map/all_gather | solution.py:92
  176.1 5.5 %fusion.17 = f32[768,384]{1,0:T(8,128)S(1)} fusion(f32[768,768]{1,0:T(8,128)} %all-gather.7.cloned.1.call-done, f32[768,384]{1,0:T(8,128)S(1)} %get-tuple-element.137), kind=kOutput, calls=%fused_computation.63 | convolution fusion | flops 2717908992 | bytes 4718592 | tf_op jit(solution)/shard_map/dot_general | solution.py:23
  181.6 2.5 collective-permute-start.1
  184.1 51.3 %collective-permute-done.1 = f32[768,384]{1,0:T(8,128)S(1)} collective-permute-done((f32[768,384]{1,0:T(8,128)S(1)}, f32[768,384]{1,0:T(8,128)S(1)}, u32[]{:S(2)}, u32[]{:S(2)}) %collective-permute-start.1) | collective-permute-done | bytes 1179680 | tf_op jit(solution)/shard_map/ppermute | solution.py:13
  235.4 1.0 copy-done.6
  236.5 36.1 %all-gather.9.cloned.1.call-done = f32[768,768]{1,0:T(8,128)} async-done(((f32[768,384]{1,0:T(8,128)}), f32[768,768]{1,0:T(8,128)}) %all-gather.9.cloned.1.call-update) | async-done | bytes 2359312 | tf_op jit(solution)/shard_map/all_gather | solution.py:92
  272.6 5.5 %fusion.15 = (f32[384]{0:T(512)S(1)}, f32[768,384]{1,0:T(8,128)S(1)}) fusion(f32[768,768]{1,0:T(8,128)} %all-gather.9.cloned.1.call-done, f32[768,384]{1,0:T(8,128)S(1)} %fusion.17), kind=kOutput, calls=%fused_computation.61 | convolution fusion | flops 2718203392 | bytes 4720128 | tf_op jit(solution)/shard_map/dot_general | solution.py:23
  278.1 0.6 reduce_max.9
  278.7 5.5 %pmax.7 = f32[]{:T(128)} all-reduce(f32[]{:T(128)} %reduce_max.9), channel_id=1, replica_groups=mesh['grp'=2,'tm'=4,'spin'=2,'rows'=2] {'rows'}, use_global_device_ids=true, to_apply=%region_7.8 | all-reduce | flops 1 | bytes 8 | tf_op jit(solution)/shard_map/pmax | solution.py:93
  284.9 1.1 broadcast_divide_fusion
  286.1 36.2 %all-gather.11.cloned.1.call-done = f32[768,768]{1,0:T(8,128)} async-done(((f32[768,384]{1,0:T(8,128)}), f32[768,768]{1,0:T(8,128)}) %all-gather.11.cloned.1.call-update) | async-done | bytes 2359312 | tf_op jit(solution)/shard_map/all_gather | solution.py:105
  322.2 6.5 %fusion.18 = f32[768,384]{1,0:T(8,128)} fusion(f32[768,768]{1,0:T(8,128)} %all-gather.11.cloned.1.call-done, f32[768,384]{1,0:T(8,128)S(1)} %copy-done.1), kind=kOutput, calls=%fused_computation.64 | convolution fusion | flops 2717908992 | bytes 4718592 | tf_op jit(solution)/shard_map/dot_general | solution.py:23
  328.8 36.2 %all-gather.13.cloned.1.call-done = f32[768,768]{1,0:T(8,128)} async-done(((f32[768,384]{1,0:T(8,128)}), f32[768,768]{1,0:T(8,128)}) %all-gather.13.cloned.1.call-update) | async-done | bytes 2359312 | tf_op jit(solution)/shard_map/all_gather | solution.py:105
  365.0 6.5 %fusion.19 = f32[768,384]{1,0:T(8,128)} fusion(f32[768,768]{1,0:T(8,128)} %all-gather.13.cloned.1.call-done, f32[768,384]{1,0:T(8,128)S(1)} %copy-done.2), kind=kOutput, calls=%fused_computation.65 | convolution fusion | flops 2717908992 | bytes 4718592 | tf_op jit(solution)/shard_map/dot_general | solution.py:23
  371.5 0.3 all-gather.17.cloned.1.call-start
  371.8 35.9 %all-gather.15.cloned.1.call-done = f32[768,768]{1,0:T(8,128)} async-done(((f32[768,384]{1,0:T(8,128)}), f32[768,768]{1,0:T(8,128)}) %all-gather.15.cloned.1.call-update) | async-done | bytes 2359312 | tf_op jit(solution)/shard_map/all_gather | solution.py:105
  407.7 6.5 %fusion.20 = f32[768,384]{1,0:T(8,128)} fusion(f32[768,768]{1,0:T(8,128)} %all-gather.15.cloned.1.call-done, f32[768,384]{1,0:T(8,128)S(1)} %copy-done.3), kind=kOutput, calls=%fused_computation.66 | convolution fusion | flops 2717908992 | bytes 4718592 | tf_op jit(solution)/shard_map/dot_general | solution.py:23
  414.3 5.7 %convolution_add_fusion.2 = f32[768,384]{1,0:T(8,128)S(1)} fusion(f32[768,768]{1,0:T(8,128)} %all-gather.13.cloned.1.call-done, f32[768,384]{1,0:T(8,128)S(1)} %copy-done.1, s32[384]{0:T(512)S(1)} %iota_add_fusion), kind=kOutput, calls=%fused_computation.16 | convolution fusion | flops 2719088640 | bytes 4720128 | tf_op jit(solution)/shard_map/dot_general | solution.py:23
  420.0 3.9 convolution_add_fusion.1
  423.9 26.6 %all-gather.17.cloned.1.call-done = f32[768,768]{1,0:T(8,128)} async-done(((f32[768,384]{1,0:T(8,128)}), f32[768,768]{1,0:T(8,128)}) %all-gather.17.cloned.1.call-update) | async-done | bytes 2359312 | tf_op jit(solution)/shard_map/all_gather | solution.py:105
  450.5 5.5 %convolution_add_fusion = f32[768,384]{1,0:T(8,128)S(1)} fusion(f32[768,384]{1,0:T(8,128)S(1)} %convolution_add_fusion.1, f32[768,768]{1,0:T(8,128)} %all-gather.17.cloned.1.call-done), kind=kOutput, calls=%fused_computation.14 | convolution fusion | flops 2718203904 | bytes 4718592 | tf_op jit(solution)/shard_map/dot_general | solution.py:23
  456.0 2.8 collective-permute-done.2
  458.9 0.4 copy.17
  459.3 18.0 %all_to_all.19 = f32[2,384,384]{1,2,0:T(8,128)S(1)} all-to-all(f32[2,384,384]{1,2,0:T(8,128)S(1)} %copy.17), channel_id=1, replica_groups=mesh['grp'=2,'tm'=4,'spin'=2,'rows'=2] {'rows'}, dimensions={0} | all-to-all | bytes 2359296 | tf_op jit(solution)/shard_map/all_to_all | solution.py:112
  477.3 1.2 fusion.1
  (48 shorter events, 0.8 us)
Async XLA Ops:
  6.5 169.5 %all-gather.7.cloned.1.call-start = ((), (), s32[]{:S(2)}) async-start(), calls=%async_computation.1 | async-start | bytes 3538944 | tf_op jit(solution)/shard_map/all_gather | solution.py:92
  9.9 13.5 %copy-start.10 = (f32[3072]{0:T(1024)S(1)}, f32[3072]{0:T(1024)}, u32[]{:S(2)}) copy-start(f32[3072]{0:T(1024)} %param.8) | copy-start | bytes 36868
  63.3 1.9 copy-start.9
  65.2 0.6 copy-start.8
  71.7 3.4 copy-start.7
  75.1 1.0 copy-start
  85.6 1.0 copy-start
  96.1 1.0 copy-start
  106.6 30.4 %collective-permute-start = (f32[768,384]{1,0:T(8,128)S(1)}, f32[768,384]{1,0:T(8,128)S(1)}, u32[]{:S(2)}, u32[]{:S(2)}) collective-permute-start(f32[768,384]{1,0:T(8,128)S(1)} %get-tuple-element.137), channel_id=1, source_target_pairs={{0,12},{4,0},{8,4},{12,8},{1,13},{5,1},{9,5},{13,9},{2,14},{6,2},{... | collective-permute-start | bytes 3538952 | tf_op jit(solution)/shard_map/ppermute | solution.py:13
  136.9 1.0 copy-start.5
  138.0 134.6 %all-gather.9.cloned.1.call-start = ((), (), s32[]{:S(2)}) async-start(), calls=%async_computation.2 | async-start | bytes 3538944 | tf_op jit(solution)/shard_map/all_gather | solution.py:92
  181.6 53.8 %collective-permute-start.1 = (f32[768,384]{1,0:T(8,128)S(1)}, f32[768,384]{1,0:T(8,128)S(1)}, u32[]{:S(2)}, u32[]{:S(2)}) collective-permute-start(f32[768,384]{1,0:T(8,128)S(1)} %fusion.17), channel_id=1, source_target_pairs={{0,8},{4,12},{8,0},{12,4},{1,9},{5,13},{9,1},{13,5},{2,10},{6,14},... | collective-permute-start | bytes 3538952 | tf_op jit(solution)/shard_map/ppermute | solution.py:13
  235.4 1.0 copy-start.6
  236.4 85.8 %all-gather.11.cloned.1.call-start = ((), (), s32[]{:S(2)}) async-start(), calls=%async_computation.3 | async-start | bytes 3538944 | tf_op jit(solution)/shard_map/all_gather | solution.py:105
  286.0 36.2 %copy-start.1 = (f32[768,384]{1,0:T(8,128)S(1)}, f32[768,384]{1,0:T(8,128)}, u32[]{:S(2)}) copy-start(f32[768,384]{1,0:T(8,128)} %broadcast_divide_fusion) | copy-start | bytes 3538948
  286.0 79.0 %all-gather.13.cloned.1.call-start = ((), (), s32[]{:S(2)}) async-start(), calls=%async_computation.4 | async-start | bytes 3538944 | tf_op jit(solution)/shard_map/all_gather | solution.py:105
  328.7 36.2 %copy-start.2 = (f32[768,384]{1,0:T(8,128)S(1)}, f32[768,384]{1,0:T(8,128)}, u32[]{:S(2)}) copy-start(f32[768,384]{1,0:T(8,128)} %fusion.18) | copy-start | bytes 3538948
  328.8 78.9 %all-gather.15.cloned.1.call-start = ((), (), s32[]{:S(2)}) async-start(), calls=%async_computation.5 | async-start | bytes 3538944 | tf_op jit(solution)/shard_map/all_gather | solution.py:105
  371.5 36.2 %copy-start.3 = (f32[768,384]{1,0:T(8,128)S(1)}, f32[768,384]{1,0:T(8,128)}, u32[]{:S(2)}) copy-start(f32[768,384]{1,0:T(8,128)} %fusion.19) | copy-start | bytes 3538948
  371.5 78.9 %all-gather.17.cloned.1.call-start = ((), (), s32[]{:S(2)}) async-start(), calls=%async_computation.6 | async-start | bytes 3538944 | tf_op jit(solution)/shard_map/all_gather | solution.py:105
  414.3 5.7 %copy-start.4 = (f32[768,768]{1,0:T(8,128)S(1)}, f32[768,768]{1,0:T(8,128)}, u32[]{:S(2)}) copy-start(f32[768,768]{1,0:T(8,128)} %all-gather.15.cloned.1.call-done) | copy-start | bytes 7077892
  456.0 2.9 collective-permute-start.2
Sparse Core Ops, SparseCore 0:
  138.1 37.9 all-gather.6
  236.5 36.0 all-gather.8
  286.1 36.0 all-gather.10
  328.9 36.0 all-gather.12
  371.6 36.0 all-gather.14
  414.4 36.0 all-gather.16
where the time goes:
time: 487 us; the launch traced here: 485 us
  waiting for transfers between devices  288 us (59%)
  matrix products  61.3 us (13%)
  other arithmetic  49.2 us (10%)
  local copies, waits for them, and re-layouts  40.3 us (8%)
  blocking collectives  23.6 us (5%)
  between operations  14.3 us (3%)
  starting transfers between devices  8.29 us (2%)
    all_gather x4, waiting for transfers between devices, per_device(): lax.all_gather(power, 'rows', axis=1, tiled=True)  135 us
    ppermute x2, waiting for transfers between devices, from_behind(): return lax.ppermute(x, axis, [(i, (i + by) % size) for i in range(size)])  76.5 us
    all_gather x2, waiting for transfers between devices, per_device(): lax.all_gather(distant, 'rows', axis=1, tiled=True)  74 us
    dot_general x8, matrix products, matmul_hi(): jnp.dot(left, right, precision=lax.Precision.HIGHEST, preferred_element_t...  45.6 us
    unnamed x5, other arithmetic  35.9 us
    all_to_all x1, blocking collectives, per_device(): lax.all_to_all(partner, 'rows', split_axis=0, concat_axis=1, tiled=True)  18 us
    dot_general x3, matrix products, slice_step(): jnp.einsum('rjab,rjbc->rac', k_tiles, gathered, precision=lax.Precision.H...  15.6 us
    gather x1, local copies, waits for them, and re-layouts, build_kinetic(): kept_mask = tile_mask[site_from // tile_len, site_to // tile_len]  13.4 us
  transfers between devices with their start and end apart: 9, of which 9 were waited for; matrix products, arithmetic and copies ran while one was open for 2% of the time, Pallas kernels for 0%

commit v1 on v0

v1 whole, which is shorter than its diff:
```python
import functools
import math

import jax
import jax.numpy as jnp
from jax import lax
from jax.experimental import pallas as pl
from jax.experimental.pallas import tpu as pltpu
from jax.sharding import PartitionSpec as P

F32 = jnp.float32
BF16 = jnp.bfloat16


def dot(left, right):
    return jnp.dot(left, right, preferred_element_type=F32)


def split(x):
    high = x.astype(BF16)
    return high, (x - high.astype(F32)).astype(BF16)


def cycle_order(tile_cols_ref, n_tiles):
    order = [jnp.int32(0), tile_cols_ref[0, 1]]
    while len(order) < n_tiles:
        before, here = order[-2], order[-1]
        one, two = tile_cols_ref[here, 1], tile_cols_ref[here, 2]
        order.append(jnp.where(one == before, two, one))
    return order


def tile_ds(tile, tile_len):
    return pl.ds(pl.multiple_of(tile * tile_len, tile_len), tile_len)


def kinetic_kernel(n_tiles, tile_len, scale, tile_cols_ref, sites_ref, hopping_ref, weight_ref, acc_ref):
    order = cycle_order(tile_cols_ref, n_tiles)
    shift = tile_len.bit_length() - 1
    bonds = sites_ref.shape[1]
    pair_len = 2 * tile_len
    chunk = min(bonds, 512)

    def position(site):
        tile = site >> shift
        place = jnp.zeros_like(site)
        for p in range(1, n_tiles):
            place = jnp.where(tile == order[p], p, place)
        return place, place * tile_len + (site & (tile_len - 1))

    acc_ref[...] = jnp.zeros_like(acc_ref)

    def add_bonds(step, carry):
        lanes = pl.ds(pl.multiple_of(step * chunk, chunk), chunk)
        tile_a, site_a = position(sites_ref[0:1, lanes])
        tile_b, site_b = position(sites_ref[1:2, lanes])
        apart = jnp.abs(tile_a - tile_b)
        kept = (apart <= 1) | (apart == n_tiles - 1)
        weight = jnp.where(kept, hopping_ref[0:1, lanes] * scale, 0.0)
        weight_high = weight.astype(BF16).astype(F32)
        weight_low = weight - weight_high
        swap = ((tile_a >> 1) != (tile_b >> 1)) & ((tile_a & 1) == 0)
        first = jnp.where(swap, site_b, site_a)
        second = jnp.where(swap, site_a, site_b)
        row_ids = lax.broadcasted_iota(jnp.int32, (tile_len, chunk), 0)
        rows_of, high_of, low_of = [], [], []
        for p in range(n_tiles):
            ids = row_ids + p * tile_len
            rows_of.append(jnp.where(first == ids, 1.0, 0.0).astype(BF16))
            hit = second == ids
            high_of.append(jnp.where(hit, weight_high, 0.0).astype(BF16))
            low_of.append(jnp.where(hit, weight_low, 0.0).astype(BF16))
        for pair in range(n_tiles // 2):
            left = jnp.concatenate([rows_of[(2 * pair - 1) % n_tiles], rows_of[2 * pair], rows_of[2 * pair + 1]], axis=0)
            right_high = jnp.concatenate([high_of[2 * pair], high_of[2 * pair + 1]], axis=0)
            right_low = jnp.concatenate([low_of[2 * pair], low_of[2 * pair + 1]], axis=0)
            acc_ref[pair] += lax.dot_general(
                jnp.concatenate([left, left], axis=1),
                jnp.concatenate([right_high, right_low], axis=1),
                (((1,), (1,)), ((), ())),
                preferred_element_type=F32,
            )
        return carry

    lax.fori_loop(0, bonds // chunk, add_bonds, 0)
    same = lax.broadcasted_iota(jnp.int32, (pair_len, pair_len), 0) == lax.broadcasted_iota(jnp.int32, (pair_len, pair_len), 1)
    zero = jnp.zeros((tile_len, tile_len), BF16)
    n_pairs = n_tiles // 2
    for pair in range(n_pairs):
        inner = acc_ref[pair, tile_len:, :]
        middle = split(inner + inner.T + jnp.where(same, 1.0, 0.0))
        above = split(acc_ref[pair, :tile_len, :tile_len])
        below = split(acc_ref[(pair + 1) % n_pairs, :tile_len, :tile_len].T)
        for part in range(2):
            base = part * 2 * pair_len
            weight_ref[pair, base : base + tile_len, :] = jnp.concatenate([above[part], zero], axis=1)
            weight_ref[pair, base + tile_len : base + tile_len + pair_len, :] = middle[part]
            weight_ref[pair, base + tile_len + pair_len : base + 2 * pair_len, :] = jnp.concatenate([zero, below[part]], axis=1)


def green_kernel(
    n_tiles, tile_len, coupling, tile_cols_ref, where_ref, field_ref, weight_ref,
    out_ref, factor_ref, z_ref, a_ref, b_ref, c_ref, d_ref, low_ref,
):
    order = cycle_order(tile_cols_ref, n_tiles)
    slices, matrix_order = field_ref.shape
    n_pairs = n_tiles // 2
    pair_len = 2 * tile_len
    sign = 1.0 - 2.0 * where_ref[0].astype(F32)
    for p in range(n_tiles):
        spins_pm = (2 * field_ref[:, tile_ds(order[p], tile_len)] - 1).astype(F32)
        factor_ref[:, p * tile_len : (p + 1) * tile_len] = jnp.exp(sign * coupling * spins_pm)

    for p in range(n_tiles):
        row = factor_ref[slices - 1 : slices, p * tile_len : (p + 1) * tile_len]
        column = jnp.broadcast_to(row, (tile_len, tile_len)).T
        column = jnp.concatenate([column, column], axis=1)
        for pair in range(n_pairs):
            slots = [(2 * pair - 1) % n_tiles, 2 * pair, 2 * pair + 1, (2 * pair + 2) % n_tiles]
            cell = jnp.zeros((tile_len, pair_len), F32)
            if p in slots:
                at = slots.index(p) * tile_len
                high = weight_ref[pair, at : at + tile_len, :].astype(F32)
                low = weight_ref[pair, 2 * pair_len + at : 2 * pair_len + at + tile_len, :].astype(F32)
                cell = column * (high + low)
            z_ref[p * tile_len : (p + 1) * tile_len, pair * pair_len : (pair + 1) * pair_len] = cell

    def near(x, pair):
        tiles = [(2 * pair - 1) % n_tiles, 2 * pair, 2 * pair + 1, (2 * pair + 2) % n_tiles]
        return [x[:, t * tile_len : (t + 1) * tile_len] for t in tiles]

    block = 2 * tile_len

    def slice_step(step, carry):
        factor = factor_ref[pl.ds(slices - 2 - step, 1), :]
        for start in range(0, matrix_order, block):
            high, low = split(z_ref[start : start + block, :] * factor)
            for pair in range(n_pairs):
                left = jnp.concatenate(near(high, pair) + near(low, pair) + near(high, pair), axis=1)
                whole = weight_ref[pair]
                right = jnp.concatenate([whole[: 2 * pair_len], whole], axis=0)
                z_ref[start : start + block, pair * pair_len : (pair + 1) * pair_len] = dot(left, right)
        return carry

    lax.fori_loop(0, slices - 1, slice_step, 0)

    col_max = jnp.max(jnp.sum(z_ref[...], axis=0, keepdims=True), axis=1, keepdims=True)
    z_ref[...] = z_ref[...] * (0.5 / col_max)
    p_high, p_low = split(z_ref[...])
    a_ref[...] = p_high
    low_ref[...] = p_low
    b_ref[...] = dot(a_ref[...], a_ref[...]).astype(BF16)
    d_ref[...] = dot(b_ref[...], b_ref[...]).astype(BF16)
    c_ref[...] = (b_ref[...].astype(F32) - z_ref[...] - dot(b_ref[...], a_ref[...])).astype(BF16)
    start_y = -(c_ref[...].astype(F32) + d_ref[...].astype(F32) + dot(c_ref[...], d_ref[...]))
    b_ref[...] = start_y.astype(BF16)
    for start in range(0, matrix_order, block):
        rows = slice(start, start + block)
        guess = b_ref[rows, :]
        residual = guess.astype(F32) - z_ref[rows, :] + (dot(guess, a_ref[...]) + dot(guess, low_ref[...]))
        y = guess.astype(F32) - residual + dot(residual.astype(BF16), b_ref[...])
        for i in range(block // tile_len):
            p = start // tile_len + i
            for q in range(n_tiles):
                out_ref[tile_ds(order[p], tile_len), tile_ds(order[q], tile_len)] = y[
                    i * tile_len : (i + 1) * tile_len, q * tile_len : (q + 1) * tile_len
                ]


def gather_blocks(field, axis):
    size = lax.axis_size(axis)
    held, count = [field], 1
    while count < size:
        grown = list(held)
        for step in range(1, 4):
            by = step * count
            if by >= size:
                break
            pairs = [((i + by) % size, i) for i in range(size)]
            packed = held[0] if len(held) == 1 else jnp.concatenate(held, axis=0)
            moved = lax.ppermute(packed, axis, pairs)
            grown.append(moved)
        held = grown
        count = min(size, count * 4)
        held = [jnp.concatenate(held, axis=0)]
    return held[0]


def per_device(ising_field, bond_sites, hopping, tile_cols):
    slices_here, matrix_order = ising_field.shape
    n_tiles = tile_cols.shape[0]
    tile_len = matrix_order // n_tiles
    pair_len = 2 * tile_len
    n_pairs = n_tiles // 2
    col_width = matrix_order // lax.axis_size("rows")
    total_slices = slices_here * lax.axis_size("tm")
    coupling = 1.5 / math.sqrt(total_slices)
    smem = pl.BlockSpec(memory_space=pltpu.SMEM)
    vmem = pl.BlockSpec(memory_space=pltpu.VMEM)
    field = gather_blocks(ising_field, "tm")
    weights = pl.pallas_call(
        functools.partial(kinetic_kernel, n_tiles, tile_len, 0.5 / total_slices),
        out_shape=jax.ShapeDtypeStruct((n_pairs, 4 * pair_len, pair_len), BF16),
        in_specs=[smem, vmem, vmem],
        out_specs=vmem,
        scratch_shapes=[pltpu.VMEM((n_pairs, tile_len + pair_len, pair_len), F32)],
        cost_estimate=pl.CostEstimate(flops=4 * 10**9, bytes_accessed=4 * 10**6, transcendentals=0),
        name="kinetic",
    )(tile_cols, bond_sites.T, hopping[None, :])
    where = lax.axis_index("spin").astype(jnp.int32)[None]
    square = (matrix_order, matrix_order)
    y = pl.pallas_call(
        functools.partial(green_kernel, n_tiles, tile_len, coupling),
        out_shape=jax.ShapeDtypeStruct(square, F32),
        in_specs=[smem, smem, vmem, vmem],
        out_specs=vmem,
        scratch_shapes=[pltpu.VMEM((total_slices, matrix_order), F32), pltpu.VMEM(square, F32)] + [pltpu.VMEM(square, BF16)] * 5,
        cost_estimate=pl.CostEstimate(flops=4 * 10**10, bytes_accessed=6 * 10**6, transcendentals=0),
        name="green",
    )(tile_cols, where, field, weights)
    offset = lax.axis_index("rows") * col_width
    own_rows = lax.dynamic_slice_in_dim(y, offset, col_width, 0)
    size = lax.axis_size("spin")
    other_rows = lax.ppermute(own_rows, "spin", [(i, (i + 1) % size) for i in range(size)])
    own_cols = lax.dynamic_slice_in_dim(y, offset, col_width, 1)
    row_ids = jnp.arange(matrix_order, dtype=jnp.int32)[:, None]
    col_ids = offset + jnp.arange(col_width, dtype=jnp.int32)[None, :]
    eye_cols = (row_ids == col_ids).astype(F32)
    xcorr = (eye_cols - own_cols) * other_rows.T
    return xcorr[None, None]


def solution(mesh):
    placed = (P(("grp", "tm"), None), P(), P(), P())
    return jax.shard_map(
        per_device,
        mesh=mesh,
        in_specs=placed,
        out_specs=P("spin", ("grp", "tm"), None, "rows"),
        check_vma=False,
    )
```

time: 487 us -> 63.8 us (0.13)
  waiting for transfers between devices: 288 us -> 2.59 us
  matrix products: 61.3 us -> 0 us
  other arithmetic: 49.2 us -> 0.87 us
  Pallas kernels: 0 us -> 48.3 us
  local copies, waits for them, and re-layouts: 40.3 us -> 5.71 us
  blocking collectives: 23.6 us -> 0 us
  between operations: 14.3 us -> 0.05 us
    all_gather x6 -> x0, waiting for transfers between devices: 209 us -> none  [the longest x4 135 us: per_device(): lax.all_gather(power, 'rows', axis=1, tiled=True)]
    ppermute x3 -> x4, waiting for transfers between devices: 79.4 us -> 2.59 us  [the longest x1 2.58 us: per_device(): lax.ppermute(own_rows, 'spin', [(i, (i + 1) % size) for i in range(size)])]
    dot_general x11 -> x0, matrix products: 61.3 us -> none  [the longest x8 45.6 us: matmul_hi(): jnp.dot(left, right, precision=lax.Precision.HIGHEST, preferred_element_t...]
    pallas_call x0 -> x2, Pallas kernels: none -> 48.3 us  [the longest x1 40.8 us: per_device(): pl.pallas_call(functools.partial(green_kernel, n_tiles, tile_len, couplin...]
    unnamed x5 -> x0, other arithmetic: 35.9 us -> none
    gather x5 -> x0, local copies, waits for them, and re-layouts: 23 us -> none  [the longest x1 13.4 us: build_kinetic(): kept_mask = tile_mask[site_from // tile_len, site_to // tile_len]]
    all_to_all x1 -> x0, blocking collectives: 18 us -> none  [per_device(): lax.all_to_all(partner, 'rows', split_axis=0, concat_axis=1, tiled=True)]
    mul x6 -> x0, other arithmetic: 6.05 us -> none  [the longest x3 4.31 us: slice_step(): factors[slice_pos][:, None] * product.reshape(matrix_order, col_width)]
  transfers between devices with their start and end apart: 9 -> 4, of which waited for: 9 -> 1; matrix products, arithmetic and copies ran while one was open for 2% -> 3% of each run, Pallas kernels for 0% -> 12%
where the time goes in v1:
time: 63.8 us; the launch traced here: 63.6 us
  Pallas kernels  48.3 us (76%)
  starting transfers between devices  6.09 us (10%)
  local copies, waits for them, and re-layouts  5.71 us (9%)
  waiting for transfers between devices  2.59 us (4%)
  other arithmetic  0.87 us (1%)
    pallas_call x1, Pallas kernels, per_device(): pl.pallas_call(functools.partial(green_kernel, n_tiles, tile_len, couplin...  40.8 us
    pallas_call x1, Pallas kernels, per_device(): pl.pallas_call(functools.partial(kinetic_kernel, n_tiles, tile_len, 0.5 /...  7.51 us
    ppermute x3, starting transfers between devices, gather_blocks(): moved = lax.ppermute(packed, axis, pairs)  6.09 us
    ppermute x1, waiting for transfers between devices, per_device(): lax.ppermute(own_rows, 'spin', [(i, (i + 1) % size) for i in range(size)])  2.58 us
    dynamic_slice x1, local copies, waits for them, and re-layouts, per_device(): own_rows = lax.dynamic_slice_in_dim(y, offset, col_width, 0)  2.51 us
    unnamed x6, local copies, waits for them, and re-layouts  1.73 us
    broadcast_in_dim x1, local copies, waits for them, and re-layouts, per_device(): return xcorr[None, None]  1.38 us
  transfers between devices with their start and end apart: 4, of which 1 were waited for; matrix products, arithmetic and copies ran while one was open for 3% of the time, Pallas kernels for 12%

profile of v1, /device:TPU:0, one launch (start us, length us, event | category | flops | bytes accessed | tf_op | source)
XLA Modules:
  0.0 63.6 jit_solution(14462689644898144441)
XLA Ops:
  0.0 4.1 %collective-permute-start.1 = (s32[4,768]{1,0:T(4,128)}, s32[4,768]{1,0:T(4,128)S(1)}, u32[]{:S(2)}, u32[]{:S(2)}) collective-permute-start(s32[4,768]{1,0:T(4,128)} %param.4), channel_id=1, source_target_pairs={{8,0},{12,4},{0,8},{4,12},{9,1},{13,5},{1,9},{5,13},{10,2},{14,6},... | collective-permute-start | bytes 36872 | tf_op jit(solution)/shard_map/ppermute | solution.py:181
  4.1 1.3 %collective-permute-start = (s32[4,768]{1,0:T(4,128)}, s32[4,768]{1,0:T(4,128)S(1)}, u32[]{:S(2)}, u32[]{:S(2)}) collective-permute-start(s32[4,768]{1,0:T(4,128)} %param.4), channel_id=1, source_target_pairs={{4,0},{8,4},{12,8},{0,12},{5,1},{9,5},{13,9},{1,13},{6,2},{10,6},{... | collective-permute-start | bytes 36872 | tf_op jit(solution)/shard_map/ppermute | solution.py:181
  5.4 0.7 %collective-permute-start.2 = (s32[4,768]{1,0:T(4,128)}, s32[4,768]{1,0:T(4,128)S(1)}, u32[]{:S(2)}, u32[]{:S(2)}) collective-permute-start(s32[4,768]{1,0:T(4,128)} %param.4), channel_id=1, source_target_pairs={{12,0},{0,4},{4,8},{8,12},{13,1},{1,5},{5,9},{9,13},{14,2},{2,6},{... | collective-permute-start | bytes 36872 | tf_op jit(solution)/shard_map/ppermute | solution.py:181
  6.1 1.4 %copy.6.tile_cols_ref = s32[6,3]{1,0:T(8,128)} copy(s32[6,3]{0,1:T(4,128)} %param.7) | data formatting | bytes 144 | tf_op args[3]
  7.4 0.0 copy-start.1
  7.5 7.5 %kinetic.1.weight_ref = bf16[3,1024,256]{2,1,0:T(8,128)(2,1)} custom-call(s32[6,3]{1,0:T(8,128)} %copy.6.tile_cols_ref, s32[2,3072]{1,0:T(2,128)} %bitcast.9, f32[1,3072]{1,0:T(1,128)} %bitcast.10), custom_call_target="tpu_custom_call" | custom-call | flops 4000000000 | bytes 4000000 | tf_op jit(solution)/shard_map/kinetic/pallas_call | solution.py:201
  15.0 0.0 collective-permute-done.1
  15.0 0.0 collective-permute-done
  15.0 0.0 collective-permute-done.2
  15.0 0.0 copy-done.1
  15.0 0.6 %pad_add_fusion.field_ref = s32[16,768]{1,0:T(8,128)} fusion(s32[4,768]{1,0:T(4,128)S(1)} %collective-permute-done.2, s32[4,768]{1,0:T(4,128)S(1)} %collective-permute-done.1, s32[4,768]{1,0:T(4,128)S(1)} %collective-permute-done, s32[4,768]{1,0:T(4,128)S(1)} %copy-done.1), kind=kLoop, calls=%fused_computation.3 | loop fusion | flops 36864 | bytes 98304 | tf_op jit(solution)/shard_map/concatenate | solution.py:185
  15.6 40.8 %green.1 = f32[768,768]{1,0:T(8,128)} custom-call(s32[6,3]{1,0:T(8,128)} %copy.6.tile_cols_ref, s32[1]{0:T(128)} %bitcast.where_ref, s32[16,768]{1,0:T(8,128)} %pad_add_fusion.field_ref, bf16[3,1024,256]{2,1,0:T(8,128)(2,1)} %kinetic.1.weight_ref), custom_call_target="tpu_custom_call" | custom-call | flops 40000000000 | bytes 6000000 | tf_op jit(solution)/shard_map/green/pallas_call | solution.py:212
  56.4 0.0 copy-start
  56.4 2.5 %constant_dynamic-slice_fusion = f32[384,768]{1,0:T(8,128)} fusion(f32[768,768]{1,0:T(8,128)} %green.1, s32[]{:T(128)S(6)} %select_n.4), kind=kLoop, calls=%fused_computation.5 | loop fusion | bytes 2359300 | tf_op jit(solution)/shard_map/dynamic_slice | solution.py:222
  58.9 0.0 collective-permute-start.3
  58.9 0.0 copy-done
  58.9 0.1 constant_dynamic-slice_fusion.1
  59.0 0.4 copy.9
  59.4 2.6 %collective-permute-done.3 = f32[384,768]{1,0:T(8,128)S(1)} collective-permute-done((f32[384,768]{1,0:T(8,128)}, f32[384,768]{1,0:T(8,128)S(1)}, u32[]{:S(2)}, u32[]{:S(2)}) %collective-permute-start.3) | collective-permute-done | bytes 1179680 | tf_op jit(solution)/shard_map/ppermute | solution.py:224
  62.0 0.2 fusion
  62.2 1.4 %copy.8 = f32[1,1,768,384]{3,2,1,0:T(8,128)} copy(f32[1,1,768,384]{2,3,1,0:T(8,128)S(1)} %fusion) | data formatting | bytes 2359296 | tf_op jit(solution)/shard_map/broadcast_in_dim | solution.py:230
  (1 shorter events, 0.0 us)
Async XLA Ops:
  0.0 15.0 %collective-permute-start.1 = (s32[4,768]{1,0:T(4,128)}, s32[4,768]{1,0:T(4,128)S(1)}, u32[]{:S(2)}, u32[]{:S(2)}) collective-permute-start(s32[4,768]{1,0:T(4,128)} %param.4), channel_id=1, source_target_pairs={{8,0},{12,4},{0,8},{4,12},{9,1},{13,5},{1,9},{5,13},{10,2},{14,6},... | collective-permute-start | bytes 36872 | tf_op jit(solution)/shard_map/ppermute | solution.py:181
  4.1 10.9 %collective-permute-start = (s32[4,768]{1,0:T(4,128)}, s32[4,768]{1,0:T(4,128)S(1)}, u32[]{:S(2)}, u32[]{:S(2)}) collective-permute-start(s32[4,768]{1,0:T(4,128)} %param.4), channel_id=1, source_target_pairs={{4,0},{8,4},{12,8},{0,12},{5,1},{9,5},{13,9},{1,13},{6,2},{10,6},{... | collective-permute-start | bytes 36872 | tf_op jit(solution)/shard_map/ppermute | solution.py:181
  5.4 9.6 %collective-permute-start.2 = (s32[4,768]{1,0:T(4,128)}, s32[4,768]{1,0:T(4,128)S(1)}, u32[]{:S(2)}, u32[]{:S(2)}) collective-permute-start(s32[4,768]{1,0:T(4,128)} %param.4), channel_id=1, source_target_pairs={{12,0},{0,4},{4,8},{8,12},{13,1},{1,5},{5,9},{9,13},{14,2},{2,6},{... | collective-permute-start | bytes 36872 | tf_op jit(solution)/shard_map/ppermute | solution.py:181
  7.4 7.5 %copy-start.1 = (s32[4,768]{1,0:T(4,128)S(1)}, s32[4,768]{1,0:T(4,128)}, u32[]{:S(2)}) copy-start(s32[4,768]{1,0:T(4,128)} %param.4) | copy-start | bytes 36868
  56.4 2.5 %copy-start = (f32[768,768]{1,0:T(8,128)S(1)}, f32[768,768]{1,0:T(8,128)}, u32[]{:S(2)}) copy-start(f32[768,768]{1,0:T(8,128)} %green.1) | copy-start | bytes 7077892
  58.9 3.1 %collective-permute-start.3 = (f32[384,768]{1,0:T(8,128)}, f32[384,768]{1,0:T(8,128)S(1)}, u32[]{:S(2)}, u32[]{:S(2)}) collective-permute-start(f32[384,768]{1,0:T(8,128)} %constant_dynamic-slice_fusion), channel_id=1, source_target_pairs={{0,2},{2,0},{1,3},{3,1},{4,6},{6,4},{5,7},{7,5},{8,10},{10,8},{9,1... | collective-permute-start | bytes 3538952 | tf_op jit(solution)/shard_map/ppermute | solution.py:224

commit v2 on v1

v2 whole, which is shorter than its diff:
```python
import functools
import math

import jax
import jax.numpy as jnp
from jax import lax
from jax.experimental import pallas as pl
from jax.experimental.pallas import tpu as pltpu
from jax.sharding import PartitionSpec as P

F32 = jnp.float32
BF16 = jnp.bfloat16


def dot(left, right):
    return jnp.dot(left, right, preferred_element_type=F32)


def split(x):
    high = x.astype(BF16)
    return high, (x - high.astype(F32)).astype(BF16)


def cycle_order(tile_cols_ref, n_tiles):
    order = [jnp.int32(0), tile_cols_ref[1, 0]]
    while len(order) < n_tiles:
        before, here = order[-2], order[-1]
        one, two = tile_cols_ref[1, here], tile_cols_ref[2, here]
        order.append(jnp.where(one == before, two, one))
    return order


def place_of(order, tile):
    place = jnp.int32(0)
    for p in range(1, len(order)):
        place = jnp.where(order[p] == tile, p, place)
    return place


def tile_ds(tile, tile_len):
    return pl.ds(pl.multiple_of(tile * tile_len, tile_len), tile_len)


def kinetic_kernel(n_tiles, tile_len, scale, tile_cols_ref, sites_ref, hopping_ref, weight_ref, acc_ref):
    order = cycle_order(tile_cols_ref, n_tiles)
    shift = tile_len.bit_length() - 1
    bonds = sites_ref.shape[1]
    pair_len = 2 * tile_len
    chunk = min(bonds, 512)

    def position(site):
        tile = site >> shift
        place = jnp.zeros_like(site)
        for p in range(1, n_tiles):
            place = jnp.where(tile == order[p], p, place)
        return place, place * tile_len + (site & (tile_len - 1))

    acc_ref[...] = jnp.zeros_like(acc_ref)

    def add_bonds(step, carry):
        lanes = pl.ds(pl.multiple_of(step * chunk, chunk), chunk)
        tile_a, site_a = position(sites_ref[0:1, lanes])
        tile_b, site_b = position(sites_ref[1:2, lanes])
        apart = jnp.abs(tile_a - tile_b)
        kept = (apart <= 1) | (apart == n_tiles - 1)
        weight = jnp.where(kept, hopping_ref[0:1, lanes] * scale, 0.0)
        weight_high = weight.astype(BF16).astype(F32)
        weight_low = weight - weight_high
        swap = ((tile_a >> 1) != (tile_b >> 1)) & ((tile_a & 1) == 0)
        first = jnp.where(swap, site_b, site_a)
        second = jnp.where(swap, site_a, site_b)
        row_ids = lax.broadcasted_iota(jnp.int32, (tile_len, chunk), 0)
        high_of, low_of, ones_of = [], [], []
        for p in range(n_tiles):
            ids = row_ids + p * tile_len
            hit = first == ids
            high_of.append(jnp.where(hit, weight_high, 0.0).astype(BF16))
            low_of.append(jnp.where(hit, weight_low, 0.0).astype(BF16))
            ones_of.append(jnp.where(second == ids, 1.0, 0.0).astype(BF16))
        for pair in range(n_tiles // 2):
            tiles = [(2 * pair - 1) % n_tiles, 2 * pair, 2 * pair + 1]
            left = jnp.concatenate([high_of[t] for t in tiles] + [low_of[t] for t in tiles], axis=0)
            right = jnp.concatenate([ones_of[2 * pair], ones_of[2 * pair + 1]], axis=0)
            both = lax.dot_general(left, right, (((1,), (1,)), ((), ())), preferred_element_type=F32)
            half = tile_len + pair_len
            acc_ref[pair] += both[:half] + both[half:]
        return carry

    lax.fori_loop(0, bonds // chunk, add_bonds, 0)
    same = lax.broadcasted_iota(jnp.int32, (pair_len, pair_len), 0) == lax.broadcasted_iota(jnp.int32, (pair_len, pair_len), 1)
    zero = jnp.zeros((tile_len, tile_len), BF16)
    n_pairs = n_tiles // 2
    for pair in range(n_pairs):
        inner = acc_ref[pair, tile_len:, :]
        high, low = split(inner + inner.T + jnp.where(same, 1.0, 0.0))
        weight_ref[pair, :pair_len, :] = high
        weight_ref[pair, pair_len : 2 * pair_len, :] = low
        above = acc_ref[pair, :tile_len, :tile_len]
        below = acc_ref[(pair + 1) % n_pairs, :tile_len, :tile_len].T
        for side, cell in enumerate((above, below)):
            high, low = split(cell)
            base = (2 + side) * pair_len
            weight_ref[pair, base : base + tile_len, :] = jnp.concatenate([high, low], axis=1)
            weight_ref[pair, base + tile_len : base + pair_len, :] = jnp.concatenate([high, zero], axis=1)


def chain(n_tiles, tile_len, factor_ref, weight_ref, z_ref):
    slices, matrix_order = factor_ref.shape
    n_pairs = n_tiles // 2
    pair_len = 2 * tile_len

    for p in range(n_tiles):
        row = factor_ref[slices - 1 : slices, p * tile_len : (p + 1) * tile_len]
        column = jnp.broadcast_to(row, (tile_len, tile_len)).T
        rows = slice(p * tile_len, (p + 1) * tile_len)
        z_ref[rows, :] = jnp.zeros((tile_len, matrix_order), F32)
        own = p // 2
        at = (p % 2) * tile_len
        whole = weight_ref[own, at : at + tile_len, :].astype(F32) + weight_ref[own, pair_len + at : pair_len + at + tile_len, :].astype(F32)
        z_ref[rows, own * pair_len : (own + 1) * pair_len] = jnp.concatenate([column, column], axis=1) * whole
        if p % 2:
            into, base, to = (own + 1) % n_pairs, 2 * pair_len, 0
        else:
            into, base, to = (own - 1) % n_pairs, 3 * pair_len, tile_len
        cell = weight_ref[into, base : base + tile_len, :].astype(F32)
        to = into * pair_len + to
        z_ref[rows, to : to + tile_len] = column * (cell[:, :tile_len] + cell[:, tile_len:])

    def tile(x, t):
        t = t % n_tiles
        return x[:, t * tile_len : (t + 1) * tile_len]

    def one_slice(index):
        factor = factor_ref[pl.ds(index, 1), :]
        for start in range(0, matrix_order, tile_len):
            rows = slice(start, start + tile_len)
            high, low = split(z_ref[rows, :] * factor)
            for pair in range(n_pairs):
                lanes = slice(pair * pair_len, (pair + 1) * pair_len)
                weight = weight_ref[pair]
                inner = dot(
                    jnp.concatenate([high[:, lanes], low[:, lanes], high[:, lanes]], axis=1),
                    jnp.concatenate([weight[:pair_len], weight[:pair_len], weight[pair_len : 2 * pair_len]], axis=0),
                )
                sides = []
                for side, t in enumerate((2 * pair - 1, 2 * pair + 2)):
                    base = (2 + side) * pair_len
                    part = dot(jnp.concatenate([tile(high, t), tile(low, t)], axis=1), weight[base : base + pair_len])
                    sides.append(part[:, :tile_len] + part[:, tile_len:])
                z_ref[rows, lanes] = inner + jnp.concatenate(sides, axis=1)

    steps = slices - 1
    together = 3 if steps % 3 == 0 else 1

    def some_slices(step, carry):
        for i in range(together):
            one_slice(slices - 2 - step * together - i)
        return carry

    lax.fori_loop(0, steps // together, some_slices, 0)


def corrected(guess, p_high_rows, p_low_rows, p_high_ref, p_low_ref, guess_ref):
    guess32 = guess.astype(F32)
    p_rows = p_high_rows.astype(F32) + p_low_rows.astype(F32)
    residual = (guess32 - p_rows) + (dot(guess, p_high_ref[...]) + dot(guess, p_low_ref[...]))
    return guess32 - residual + dot(residual.astype(BF16), guess_ref[...])


def tiles_of_rows(where_ref, n_tiles, own_tiles):
    first = where_ref[1] * own_tiles
    own = [first + i for i in range(own_tiles)]
    rest = [jnp.where(first <= i, i + own_tiles, i) for i in range(n_tiles - own_tiles)]
    return own, rest


def rows_at(ref, places, tile_len):
    return jnp.concatenate([ref[tile_ds(p, tile_len), :] for p in places], axis=0)


def green_kernel(
    n_tiles, tile_len, own_tiles, coupling, tile_cols_ref, where_ref, field_ref, weight_ref,
    rows_ref, guess_ref, p_high_ref, p_low_ref, factor_ref, z_ref, b_ref, c_ref, d_ref,
):
    order = cycle_order(tile_cols_ref, n_tiles)
    matrix_order = field_ref.shape[1]
    sign = 1.0 - 2.0 * where_ref[0].astype(F32)
    for p in range(n_tiles):
        spins_pm = (2 * field_ref[:, tile_ds(order[p], tile_len)] - 1).astype(F32)
        factor_ref[:, p * tile_len : (p + 1) * tile_len] = jnp.exp(sign * coupling * spins_pm)
    chain(n_tiles, tile_len, factor_ref, weight_ref, z_ref)

    block = 2 * tile_len
    blocks = [slice(start, start + block) for start in range(0, matrix_order, block)]
    col_max = jnp.max(jnp.sum(z_ref[...], axis=0, keepdims=True), axis=1, keepdims=True)
    shrink = 0.5 / col_max
    for rows in blocks:
        p_rows = z_ref[rows, :] * shrink
        p_high_ref[rows, :], p_low_ref[rows, :] = split(p_rows)
    for rows in blocks:
        b_ref[rows, :] = dot(p_high_ref[rows, :], p_high_ref[...]).astype(BF16)
    for rows in blocks:
        square = b_ref[rows, :]
        cube = dot(square, p_high_ref[...])
        c_ref[rows, :] = (square.astype(F32) - p_high_ref[rows, :].astype(F32) - p_low_ref[rows, :].astype(F32) - cube).astype(BF16)
        d_ref[rows, :] = dot(square, b_ref[...]).astype(BF16)
    for rows in blocks:
        part = c_ref[rows, :]
        guess_ref[rows, :] = (-(part.astype(F32) + d_ref[rows, :].astype(F32) + dot(part, d_ref[...]))).astype(BF16)

    own, _ = tiles_of_rows(where_ref, n_tiles, own_tiles)
    places = [place_of(order, t) for t in own]
    y = corrected(
        rows_at(guess_ref, places, tile_len), rows_at(p_high_ref, places, tile_len), rows_at(p_low_ref, places, tile_len),
        p_high_ref, p_low_ref, guess_ref,
    )
    for q in range(n_tiles):
        rows_ref[:, tile_ds(order[q], tile_len)] = y[:, q * tile_len : (q + 1) * tile_len]


def rest_kernel(n_tiles, tile_len, own_tiles, tile_cols_ref, where_ref, guess_ref, p_high_ref, p_low_ref, out_ref, y_ref):
    order = cycle_order(tile_cols_ref, n_tiles)
    own, rest = tiles_of_rows(where_ref, n_tiles, own_tiles)
    places = [place_of(order, t) for t in rest]
    y_ref[...] = corrected(
        rows_at(guess_ref, places, tile_len), rows_at(p_high_ref, places, tile_len), rows_at(p_low_ref, places, tile_len),
        p_high_ref, p_low_ref, guess_ref,
    )
    for i, t in enumerate(own):
        out_ref[:, i * tile_len : (i + 1) * tile_len] = y_ref[:, tile_ds(place_of(order, t), tile_len)]


def xcorr_kernel(n_tiles, tile_len, own_tiles, where_ref, rows_ref, rest_ref, other_ref, out_ref):
    own, rest = tiles_of_rows(where_ref, n_tiles, own_tiles)
    width = own_tiles * tile_len
    for i, t in enumerate(own):
        rows = slice(i * tile_len, (i + 1) * tile_len)
        for j, u in enumerate(own):
            cols = slice(j * tile_len, (j + 1) * tile_len)
            green = -rows_ref[rows, tile_ds(u, tile_len)]
            if i == j:
                ids = (tile_len, tile_len)
                green += jnp.where(lax.broadcasted_iota(jnp.int32, ids, 0) == lax.broadcasted_iota(jnp.int32, ids, 1), 1.0, 0.0)
            out_ref[tile_ds(t, tile_len), cols] = green * other_ref[cols, tile_ds(t, tile_len)].T
    for i, t in enumerate(rest):
        rows = slice(i * tile_len, (i + 1) * tile_len)
        for j in range(own_tiles):
            cols = slice(j * tile_len, (j + 1) * tile_len)
            out_ref[tile_ds(t, tile_len), cols] = -rest_ref[rows, cols] * other_ref[cols, tile_ds(t, tile_len)].T


def gather_blocks(field, axis):
    size = lax.axis_size(axis)
    held, count = [field], 1
    while count < size:
        grown = list(held)
        for step in range(1, 4):
            by = step * count
            if by >= size:
                break
            pairs = [((i + by) % size, i) for i in range(size)]
            packed = held[0] if len(held) == 1 else jnp.concatenate(held, axis=0)
            moved = lax.ppermute(packed, axis, pairs)
            grown.append(moved)
        held = grown
        count = min(size, count * 4)
        held = [jnp.concatenate(held, axis=0)]
    return held[0]


def per_device(ising_field, bond_sites, hopping, tile_cols):
    slices_here, matrix_order = ising_field.shape
    n_tiles = tile_cols.shape[0]
    tile_len = matrix_order // n_tiles
    pair_len = 2 * tile_len
    n_pairs = n_tiles // 2
    n_rows = lax.axis_size("rows")
    shared = 1
    while (n_tiles * shared) % n_rows:
        shared += 1
    own_tiles = n_tiles * shared // n_rows
    own_len = own_tiles * tile_len
    col_width = matrix_order // n_rows
    total_slices = slices_here * lax.axis_size("tm")
    coupling = 1.5 / math.sqrt(total_slices)
    smem = pl.BlockSpec(memory_space=pltpu.SMEM)
    vmem = pl.BlockSpec(memory_space=pltpu.VMEM)
    field = gather_blocks(ising_field, "tm")
    cols_of_tiles = tile_cols.T
    weights = pl.pallas_call(
        functools.partial(kinetic_kernel, n_tiles, tile_len, 0.5 / total_slices),
        out_shape=jax.ShapeDtypeStruct((n_pairs, 4 * pair_len, pair_len), BF16),
        in_specs=[smem, vmem, vmem],
        out_specs=vmem,
        scratch_shapes=[pltpu.VMEM((n_pairs, tile_len + pair_len, pair_len), F32)],
        compiler_params=pltpu.CompilerParams(vmem_limit_bytes=24 * 2**20),
        cost_estimate=pl.CostEstimate(flops=4 * 10**9, bytes_accessed=4 * 10**6, transcendentals=0),
        name="kinetic",
    )(cols_of_tiles, bond_sites.T, hopping[None, :])
    where = jnp.stack([lax.axis_index("spin"), lax.axis_index("rows") // shared]).astype(jnp.int32)
    square = (matrix_order, matrix_order)
    sizes = (n_tiles, tile_len, own_tiles)
    rows, guess, p_high, p_low = pl.pallas_call(
        functools.partial(green_kernel, *sizes, coupling),
        out_shape=[jax.ShapeDtypeStruct((own_len, matrix_order), F32)] + [jax.ShapeDtypeStruct(square, BF16)] * 3,
        in_specs=[smem, smem, vmem, vmem],
        out_specs=[vmem] * 4,
        scratch_shapes=[pltpu.VMEM((total_slices, matrix_order), F32), pltpu.VMEM(square, F32)] + [pltpu.VMEM(square, BF16)] * 3,
        compiler_params=pltpu.CompilerParams(vmem_limit_bytes=32 * 2**20),
        cost_estimate=pl.CostEstimate(flops=4 * 10**10, bytes_accessed=6 * 10**6, transcendentals=0),
        name="green",
    )(cols_of_tiles, where, field, weights)
    size = lax.axis_size("spin")
    other_rows = lax.ppermute(rows, "spin", [(i, (i + 1) % size) for i in range(size)])
    rest = pl.pallas_call(
        functools.partial(rest_kernel, *sizes),
        out_shape=jax.ShapeDtypeStruct((matrix_order - own_len, own_len), F32),
        in_specs=[smem, smem, vmem, vmem, vmem],
        out_specs=vmem,
        scratch_shapes=[pltpu.VMEM((matrix_order - own_len, matrix_order), F32)],
        compiler_params=pltpu.CompilerParams(vmem_limit_bytes=24 * 2**20),
        cost_estimate=pl.CostEstimate(flops=2 * 10**9, bytes_accessed=4 * 10**6, transcendentals=0),
        name="rest",
    )(cols_of_tiles, where, guess, p_high, p_low)
    xcorr = pl.pallas_call(
        functools.partial(xcorr_kernel, *sizes),
        out_shape=jax.ShapeDtypeStruct((matrix_order, own_len), F32),
        in_specs=[smem, vmem, vmem, vmem],
        out_specs=vmem,
        compiler_params=pltpu.CompilerParams(vmem_limit_bytes=16 * 2**20),
        name="xcorr",
    )(where, rows, rest, other_rows)
    if own_len != col_width:
        xcorr = lax.dynamic_slice_in_dim(xcorr, (lax.axis_index("rows") % shared) * col_width, col_width, 1)
    return xcorr[None, None]


def solution(mesh):
    placed = (P(("grp", "tm"), None), P(), P(), P())
    return jax.shard_map(
        per_device,
        mesh=mesh,
        in_specs=placed,
        out_specs=P("spin", ("grp", "tm"), None, "rows"),
        check_vma=False,
    )
```

time: 63.8 us -> 53.2 us (0.83)
  Pallas kernels: 48.3 us -> 44.1 us
  local copies, waits for them, and re-layouts: 5.71 us -> 2.13 us
  waiting for transfers between devices: 2.59 us -> 0.44 us
  other arithmetic: 0.87 us -> 0.1 us
    pallas_call x1 -> x3, Pallas kernels: 40.8 us -> 38.1 us  [the longest x1 33.8 us: per_device(): pl.pallas_call(functools.partial(green_kernel, *sizes, coupling), out_sha...]
    dynamic_slice x2 -> x0, local copies, waits for them, and re-layouts: 2.59 us -> none  [the longest x1 2.51 us: per_device(): own_rows = lax.dynamic_slice_in_dim(y, offset, col_width, 0)]
    ppermute x1, waiting for transfers between devices: 2.58 us -> 0.44 us  [per_device(): lax.ppermute(rows, 'spin', [(i, (i + 1) % size) for i in range(size)])]
    pallas_call x1, Pallas kernels: 7.51 us -> 5.97 us  [per_device(): pl.pallas_call(functools.partial(kinetic_kernel, n_tiles, tile_len, 0.5 /...]
    broadcast_in_dim x1 -> x0, local copies, waits for them, and re-layouts: 1.38 us -> none  [per_device(): return xcorr[None, None]]
    unnamed x6 -> x10, local copies, waits for them, and re-layouts: 1.73 us -> 2.13 us
  transfers between devices with their start and end apart: 4 -> 4, of which waited for: 1 -> 1; matrix products, arithmetic and copies ran while one was open for 3% -> 0% of each run, Pallas kernels for 12% -> 16%
where the time goes in v2:
time: 53.2 us; the launch traced here: 53 us
  Pallas kernels  44.1 us (83%)
  starting transfers between devices  6.16 us (12%)
  local copies, waits for them, and re-layouts  2.13 us (4%)
    pallas_call x1, Pallas kernels, per_device(): pl.pallas_call(functools.partial(green_kernel, *sizes, coupling), out_sha...  33.8 us
    ppermute x3, starting transfers between devices, gather_blocks(): moved = lax.ppermute(packed, axis, pairs)  6.09 us
    pallas_call x1, Pallas kernels, per_device(): pl.pallas_call(functools.partial(kinetic_kernel, n_tiles, tile_len, 0.5 /...  5.97 us
    pallas_call x1, Pallas kernels, per_device(): pl.pallas_call(functools.partial(rest_kernel, *sizes), out_shape=jax.Shap...  2.39 us
    unnamed x10, local copies, waits for them, and re-layouts  2.13 us
    pallas_call x1, Pallas kernels, per_device(): pl.pallas_call(functools.partial(xcorr_kernel, *sizes), out_shape=jax.Sha...  1.94 us
  transfers between devices with their start and end apart: 4, of which 1 were waited for; matrix products, arithmetic and copies ran while one was open for 0% of the time, Pallas kernels for 16%

profile of v2, /device:TPU:0, one launch (start us, length us, event | category | flops | bytes accessed | tf_op | source)
XLA Modules:
  0.0 53.0 jit_solution(2210273018736271337)
XLA Ops:
  0.0 4.1 %collective-permute-start.1 = (s32[4,768]{1,0:T(4,128)}, s32[4,768]{1,0:T(4,128)S(1)}, u32[]{:S(2)}, u32[]{:S(2)}) collective-permute-start(s32[4,768]{1,0:T(4,128)} %param.4), channel_id=1, source_target_pairs={{8,0},{12,4},{0,8},{4,12},{9,1},{13,5},{1,9},{5,13},{10,2},{14,6},... | collective-permute-start | bytes 36872 | tf_op jit(solution)/shard_map/ppermute | solution.py:263
  4.1 1.3 %collective-permute-start = (s32[4,768]{1,0:T(4,128)}, s32[4,768]{1,0:T(4,128)S(1)}, u32[]{:S(2)}, u32[]{:S(2)}) collective-permute-start(s32[4,768]{1,0:T(4,128)} %param.4), channel_id=1, source_target_pairs={{4,0},{8,4},{12,8},{0,12},{5,1},{9,5},{13,9},{1,13},{6,2},{10,6},{... | collective-permute-start | bytes 36872 | tf_op jit(solution)/shard_map/ppermute | solution.py:263
  5.4 0.7 %collective-permute-start.2 = (s32[4,768]{1,0:T(4,128)}, s32[4,768]{1,0:T(4,128)S(1)}, u32[]{:S(2)}, u32[]{:S(2)}) collective-permute-start(s32[4,768]{1,0:T(4,128)} %param.4), channel_id=1, source_target_pairs={{12,0},{0,4},{4,8},{8,12},{13,1},{1,5},{5,9},{9,13},{14,2},{2,6},{... | collective-permute-start | bytes 36872 | tf_op jit(solution)/shard_map/ppermute | solution.py:263
  6.1 0.0 copy-start
  6.1 0.7 %copy-done = s32[3072,2]{0,1:T(2,128)S(1)} copy-done((s32[3072,2]{0,1:T(2,128)S(1)}, s32[3072,2]{0,1:T(2,128)}, u32[]{:S(2)}) %copy-start) | copy-done | bytes 24600
  6.8 0.0 copy-start.1
  6.8 0.7 %copy-done.1 = f32[3072]{0:T(1024)S(1)} copy-done((f32[3072]{0:T(1024)S(1)}, f32[3072]{0:T(1024)}, u32[]{:S(2)}) %copy-start.1) | copy-done | bytes 12312
  7.5 0.0 copy-start.2
  7.5 0.7 %copy-done.2 = s32[6,3]{0,1:T(4,128)S(1)} copy-done((s32[6,3]{0,1:T(4,128)S(1)}, s32[6,3]{0,1:T(4,128)}, u32[]{:S(2)}) %copy-start.2) | copy-done | bytes 96
  8.2 0.0 copy-start.4
  8.2 0.0 copy-start.3
  8.2 6.0 %kinetic.1.weight_ref = bf16[3,1024,256]{2,1,0:T(8,128)(2,1)S(1)} custom-call(s32[3,6]{1,0:T(4,128)S(1)} %bitcast.8, s32[2,3072]{1,0:T(2,128)S(1)} %bitcast.6, f32[1,3072]{1,0:T(1,128)S(1)} %bitcast.7), custom_call_target="tpu_custom_call" | custom-call | flops 4000000000 | bytes 4000000 | tf_op jit(solution)/shard_map/kinetic/pallas_call | solution.py:290
  14.2 0.1 pad_add_fusion.1.where_ref
  14.3 0.0 collective-permute-done.1
  14.3 0.0 collective-permute-done
  14.3 0.0 collective-permute-done.2
  14.3 0.0 copy-done.4
  14.3 0.0 copy-done.3
  14.3 33.8 %green.1 = (f32[384,768]{1,0:T(8,128)S(1)}, bf16[768,768]{1,0:T(8,128)(2,1)S(1)}, bf16[768,768]{1,0:T(8,128)(2,1)S(1)}, bf16[768,768]{1,0:T(8,128)(2,1)S(1)}) custom-call(s32[3,6]{1,0:T(4,128)S(1)} %bitcast.9, s32[2]{0:T(128)S(1)} %pad_add_fusion.1.where_ref, s32[16,768]{1,0:T(8,128)S(1)} %pad_add_fusion.field_ref, bf16[3,1024,256]{2,1,0:T(8,128)(2,1)S(1)} %kinetic.1.weight_ref), custom_call_target="tpu_custom_call" | custom-call | flops 40000000000 | bytes 6000000 | tf_op jit(solution)/shard_map/green/pallas_call | solution.py:303
  48.1 0.1 collective-permute-start.3
  48.2 2.4 %rest.1.rest_ref = f32[384,384]{1,0:T(8,128)S(1)} custom-call(s32[3,6]{1,0:T(4,128)S(1)} %bitcast.10, s32[2]{0:T(128)S(1)} %pad_add_fusion.1.where_ref, bf16[768,768]{1,0:T(8,128)(2,1)S(1)} %get-tuple-element.10.guess_ref, bf16[768,768]{1,0:T(8,128)(2,1)S(1)} %get-tuple-element.11.p_high_ref, bf16[768,768]{1,0:T(8,128)(2,1)S(1)} %get-tuple-element.12.p_low_ref), custom_call_target="tpu_custom_call" | custom-call | flops 2000000000 | bytes 4000000 | tf_op jit(solution)/shard_map/rest/pallas_call | solution.py:315
  50.6 0.4 collective-permute-done.3.other_ref
  51.0 1.9 %xcorr.1 = f32[768,384]{1,0:T(8,128)} custom-call(s32[2]{0:T(128)S(1)} %pad_add_fusion.1.where_ref, f32[384,768]{1,0:T(8,128)S(1)} %get-tuple-element.9.rows_ref, f32[384,384]{1,0:T(8,128)S(1)} %rest.1.rest_ref, f32[384,768]{1,0:T(8,128)S(1)} %collective-permute-done.3.other_ref), custom_call_target="tpu_custom_call" | custom-call | tf_op jit(solution)/shard_map/xcorr/pallas_call | solution.py:325
  (1 shorter events, 0.0 us)
Async XLA Ops:
  0.0 14.3 %collective-permute-start.1 = (s32[4,768]{1,0:T(4,128)}, s32[4,768]{1,0:T(4,128)S(1)}, u32[]{:S(2)}, u32[]{:S(2)}) collective-permute-start(s32[4,768]{1,0:T(4,128)} %param.4), channel_id=1, source_target_pairs={{8,0},{12,4},{0,8},{4,12},{9,1},{13,5},{1,9},{5,13},{10,2},{14,6},... | collective-permute-start | bytes 36872 | tf_op jit(solution)/shard_map/ppermute | solution.py:263
  4.1 10.2 %collective-permute-start = (s32[4,768]{1,0:T(4,128)}, s32[4,768]{1,0:T(4,128)S(1)}, u32[]{:S(2)}, u32[]{:S(2)}) collective-permute-start(s32[4,768]{1,0:T(4,128)} %param.4), channel_id=1, source_target_pairs={{4,0},{8,4},{12,8},{0,12},{5,1},{9,5},{13,9},{1,13},{6,2},{10,6},{... | collective-permute-start | bytes 36872 | tf_op jit(solution)/shard_map/ppermute | solution.py:263
  5.4 8.9 %collective-permute-start.2 = (s32[4,768]{1,0:T(4,128)}, s32[4,768]{1,0:T(4,128)S(1)}, u32[]{:S(2)}, u32[]{:S(2)}) collective-permute-start(s32[4,768]{1,0:T(4,128)} %param.4), channel_id=1, source_target_pairs={{12,0},{0,4},{4,8},{8,12},{13,1},{1,5},{5,9},{9,13},{14,2},{2,6},{... | collective-permute-start | bytes 36872 | tf_op jit(solution)/shard_map/ppermute | solution.py:263
  6.1 0.7 %copy-start = (s32[3072,2]{0,1:T(2,128)S(1)}, s32[3072,2]{0,1:T(2,128)}, u32[]{:S(2)}) copy-start(s32[3072,2]{0,1:T(2,128)} %param.5) | copy-start | bytes 73732
  6.8 0.7 %copy-start.1 = (f32[3072]{0:T(1024)S(1)}, f32[3072]{0:T(1024)}, u32[]{:S(2)}) copy-start(f32[3072]{0:T(1024)} %param.6) | copy-start | bytes 36868
  7.5 0.7 %copy-start.2 = (s32[6,3]{0,1:T(4,128)S(1)}, s32[6,3]{0,1:T(4,128)}, u32[]{:S(2)}) copy-start(s32[6,3]{0,1:T(4,128)} %param.7) | copy-start | bytes 220
  8.2 6.1 %copy-start.4 = (s32[4,768]{1,0:T(4,128)S(1)}, s32[4,768]{1,0:T(4,128)}, u32[]{:S(2)}) copy-start(s32[4,768]{1,0:T(4,128)} %param.4) | copy-start | bytes 36868
  8.2 6.1 %copy-start.3 = (s32[6,3]{0,1:T(4,128)S(1)}, s32[6,3]{0,1:T(4,128)}, u32[]{:S(2)}) copy-start(s32[6,3]{0,1:T(4,128)} %param.7) | copy-start | bytes 220
  48.1 2.9 %collective-permute-start.3 = (f32[384,768]{1,0:T(8,128)S(1)}, f32[384,768]{1,0:T(8,128)S(1)}, u32[]{:S(2)}, u32[]{:S(2)}) collective-permute-start(f32[384,768]{1,0:T(8,128)S(1)} %get-tuple-element.9.rows_ref), channel_id=1, source_target_pairs={{0,2},{2,0},{1,3},{3,1},{4,6},{6,4},{5,7},{7,5},{8,10},{10,8},{9,1... | collective-permute-start | bytes 3538952 | tf_op jit(solution)/shard_map/ppermute | solution.py:314

commit v3 on v2

--- a/solution.py
+++ b/solution.py
@@ -10,6 +10,7 @@
 
 F32 = jnp.float32
 BF16 = jnp.bfloat16
+F8 = jnp.float8_e4m3fn
 
 
 def dot(left, right):
@@ -41,7 +42,18 @@
     return pl.ds(pl.multiple_of(tile * tile_len, tile_len), tile_len)
 
 
-def kinetic_kernel(n_tiles, tile_len, scale, tile_cols_ref, sites_ref, hopping_ref, weight_ref, acc_ref):
+def kinetic_kernel(
+    n_tiles, tile_len, scale, tile_cols_hbm, sites_hbm, hopping_hbm, weight_ref, acc_ref, tile_cols_ref, sites_ref, hopping_ref, sems
+):
+    copies = [
+        pltpu.make_async_copy(source, target, sems.at[i])
+        for i, (source, target) in enumerate(((tile_cols_hbm, tile_cols_ref), (sites_hbm, sites_ref), (hopping_hbm, hopping_ref)))
+    ]
+    for copy in copies:
+        copy.start()
+    acc_ref[...] = jnp.zeros_like(acc_ref)
+    for copy in copies:
+        copy.wait()
     order = cycle_order(tile_cols_ref, n_tiles)
     shift = tile_len.bit_length() - 1
     bonds = sites_ref.shape[1]
@@ -55,10 +67,8 @@
             place = jnp.where(tile == order[p], p, place)
         return place, place * tile_len + (site & (tile_len - 1))
 
-    acc_ref[...] = jnp.zeros_like(acc_ref)
-
-    def add_bonds(step, carry):
-        lanes = pl.ds(pl.multiple_of(step * chunk, chunk), chunk)
+    def add_bonds(step):
+        lanes = slice(step * chunk, (step + 1) * chunk)
         tile_a, site_a = position(sites_ref[0:1, lanes])
         tile_b, site_b = position(sites_ref[1:2, lanes])
         apart = jnp.abs(tile_a - tile_b)
@@ -84,9 +94,9 @@
             both = lax.dot_general(left, right, (((1,), (1,)), ((), ())), preferred_element_type=F32)
             half = tile_len + pair_len
             acc_ref[pair] += both[:half] + both[half:]
-        return carry
-
-    lax.fori_loop(0, bonds // chunk, add_bonds, 0)
+
+    for step in range(bonds // chunk):
+        add_bonds(step)
     same = lax.broadcasted_iota(jnp.int32, (pair_len, pair_len), 0) == lax.broadcasted_iota(jnp.int32, (pair_len, pair_len), 1)
     zero = jnp.zeros((tile_len, tile_len), BF16)
     n_pairs = n_tiles // 2
@@ -142,12 +152,12 @@
                     jnp.concatenate([high[:, lanes], low[:, lanes], high[:, lanes]], axis=1),
                     jnp.concatenate([weight[:pair_len], weight[:pair_len], weight[pair_len : 2 * pair_len]], axis=0),
                 )
-                sides = []
                 for side, t in enumerate((2 * pair - 1, 2 * pair + 2)):
                     base = (2 + side) * pair_len
                     part = dot(jnp.concatenate([tile(high, t), tile(low, t)], axis=1), weight[base : base + pair_len])
-                    sides.append(part[:, :tile_len] + part[:, tile_len:])
-                z_ref[rows, lanes] = inner + jnp.concatenate(sides, axis=1)
+                    at = slice(side * tile_len, (side + 1) * tile_len)
+                    to = (2 * pair + side) * tile_len
+                    z_ref[rows, to : to + tile_len] = inner[:, at] + (part[:, :tile_len] + part[:, tile_len:])
 
     steps = slices - 1
     together = 3 if steps % 3 == 0 else 1
@@ -160,9 +170,13 @@
     lax.fori_loop(0, steps // together, some_slices, 0)
 
 
-def corrected(guess, p_high_rows, p_low_rows, p_high_ref, p_low_ref, guess_ref):
+def corrected(places, tile_len, p_high_ref, p_low_ref, guess_ref):
+    def rows_of(ref):
+        return jnp.concatenate([ref[tile_ds(p, tile_len), :] for p in places], axis=0)
+
+    guess = rows_of(guess_ref)
     guess32 = guess.astype(F32)
-    p_rows = p_high_rows.astype(F32) + p_low_rows.astype(F32)
+    p_rows = rows_of(p_high_ref).astype(F32) + rows_of(p_low_ref).astype(F32)
     residual = (guess32 - p_rows) + (dot(guess, p_high_ref[...]) + dot(guess, p_low_ref[...]))
     return guess32 - residual + dot(residual.astype(BF16), guess_ref[...])
 
@@ -174,22 +188,21 @@
     return own, rest
 
 
-def rows_at(ref, places, tile_len):
-    return jnp.concatenate([ref[tile_ds(p, tile_len), :] for p in places], axis=0)
-
-
-def green_kernel(
-    n_tiles, tile_len, own_tiles, coupling, tile_cols_ref, where_ref, field_ref, weight_ref,
-    rows_ref, guess_ref, p_high_ref, p_low_ref, factor_ref, z_ref, b_ref, c_ref, d_ref,
-):
+def chain_kernel(n_tiles, tile_len, coupling, tile_cols_ref, where_ref, field_ref, weight_ref, z_ref, factor_ref):
     order = cycle_order(tile_cols_ref, n_tiles)
-    matrix_order = field_ref.shape[1]
     sign = 1.0 - 2.0 * where_ref[0].astype(F32)
     for p in range(n_tiles):
         spins_pm = (2 * field_ref[:, tile_ds(order[p], tile_len)] - 1).astype(F32)
         factor_ref[:, p * tile_len : (p + 1) * tile_len] = jnp.exp(sign * coupling * spins_pm)
     chain(n_tiles, tile_len, factor_ref, weight_ref, z_ref)
 
+
+def green_kernel(
+    n_tiles, tile_len, own_tiles, tile_cols_ref, where_ref, z_ref,
+    rows_ref, guess_ref, p_high_ref, p_low_ref, b_ref, c_ref, one8_ref, two8_ref, part8_ref, four8_ref,
+):
+    order = cycle_order(tile_cols_ref, n_tiles)
+    matrix_order = z_ref.shape[1]
     block = 2 * tile_len
     blocks = [slice(start, start + block) for start in range(0, matrix_order, block)]
     col_max = jnp.max(jnp.sum(z_ref[...], axis=0, keepdims=True), axis=1, keepdims=True)
@@ -197,23 +210,24 @@
     for rows in blocks:
         p_rows = z_ref[rows, :] * shrink
         p_high_ref[rows, :], p_low_ref[rows, :] = split(p_rows)
+        one8_ref[rows, :] = (p_rows * 2.0**9).astype(F8)
     for rows in blocks:
-        b_ref[rows, :] = dot(p_high_ref[rows, :], p_high_ref[...]).astype(BF16)
+        square = dot(p_high_ref[rows, :], p_high_ref[...])
+        b_ref[rows, :] = square.astype(BF16)
+        two8_ref[rows, :] = (square * 2.0**10).astype(F8)
     for rows in blocks:
-        square = b_ref[rows, :]
-        cube = dot(square, p_high_ref[...])
-        c_ref[rows, :] = (square.astype(F32) - p_high_ref[rows, :].astype(F32) - p_low_ref[rows, :].astype(F32) - cube).astype(BF16)
-        d_ref[rows, :] = dot(square, b_ref[...]).astype(BF16)
+        square = two8_ref[rows, :]
+        cube = dot(square, one8_ref[...]) * 2.0**-19
+        part = b_ref[rows, :].astype(F32) - p_high_ref[rows, :].astype(F32) - cube
+        fourth = dot(square, two8_ref[...]) * 2.0**-20
+        c_ref[rows, :] = part + fourth
+        part8_ref[rows, :] = (part * 2.0**8).astype(F8)
+        four8_ref[rows, :] = (fourth * 2.0**12).astype(F8)
     for rows in blocks:
-        part = c_ref[rows, :]
-        guess_ref[rows, :] = (-(part.astype(F32) + d_ref[rows, :].astype(F32) + dot(part, d_ref[...]))).astype(BF16)
+        guess_ref[rows, :] = (-(c_ref[rows, :] + dot(part8_ref[rows, :], four8_ref[...]) * 2.0**-20)).astype(BF16)
 
     own, _ = tiles_of_rows(where_ref, n_tiles, own_tiles)
-    places = [place_of(order, t) for t in own]
-    y = corrected(
-        rows_at(guess_ref, places, tile_len), rows_at(p_high_ref, places, tile_len), rows_at(p_low_ref, places, tile_len),
-        p_high_ref, p_low_ref, guess_ref,
-    )
+    y = corrected([place_of(order, t) for t in own], tile_len, p_high_ref, p_low_ref, guess_ref)
     for q in range(n_tiles):
         rows_ref[:, tile_ds(order[q], tile_len)] = y[:, q * tile_len : (q + 1) * tile_len]
 
@@ -221,11 +235,7 @@
 def rest_kernel(n_tiles, tile_len, own_tiles, tile_cols_ref, where_ref, guess_ref, p_high_ref, p_low_ref, out_ref, y_ref):
     order = cycle_order(tile_cols_ref, n_tiles)
     own, rest = tiles_of_rows(where_ref, n_tiles, own_tiles)
-    places = [place_of(order, t) for t in rest]
-    y_ref[...] = corrected(
-        rows_at(guess_ref, places, tile_len), rows_at(p_high_ref, places, tile_len), rows_at(p_low_ref, places, tile_len),
-        p_high_ref, p_low_ref, guess_ref,
-    )
+    y_ref[...] = corrected([place_of(order, t) for t in rest], tile_len, p_high_ref, p_low_ref, guess_ref)
     for i, t in enumerate(own):
         out_ref[:, i * tile_len : (i + 1) * tile_len] = y_ref[:, tile_ds(place_of(order, t), tile_len)]
 
@@ -290,26 +300,43 @@
     weights = pl.pallas_call(
         functools.partial(kinetic_kernel, n_tiles, tile_len, 0.5 / total_slices),
         out_shape=jax.ShapeDtypeStruct((n_pairs, 4 * pair_len, pair_len), BF16),
-        in_specs=[smem, vmem, vmem],
+        in_specs=[pl.BlockSpec(memory_space=pltpu.HBM)] * 3,
         out_specs=vmem,
-        scratch_shapes=[pltpu.VMEM((n_pairs, tile_len + pair_len, pair_len), F32)],
+        scratch_shapes=[
+            pltpu.VMEM((n_pairs, tile_len + pair_len, pair_len), F32),
+            pltpu.SMEM(cols_of_tiles.shape, jnp.int32),
+            pltpu.VMEM((2, hopping.shape[0]), jnp.int32),
+            pltpu.VMEM((1, hopping.shape[0]), F32),
+            pltpu.SemaphoreType.DMA((3,)),
+        ],
         compiler_params=pltpu.CompilerParams(vmem_limit_bytes=24 * 2**20),
         cost_estimate=pl.CostEstimate(flops=4 * 10**9, bytes_accessed=4 * 10**6, transcendentals=0),
         name="kinetic",
-    )(cols_of_tiles, bond_sites.T, hopping[None, :])
+    )(*[pltpu.with_memory_space_constraint(x, pltpu.HBM) for x in (cols_of_tiles, bond_sites.T, hopping[None, :])])
     where = jnp.stack([lax.axis_index("spin"), lax.axis_index("rows") // shared]).astype(jnp.int32)
     square = (matrix_order, matrix_order)
     sizes = (n_tiles, tile_len, own_tiles)
+    product = pl.pallas_call(
+        functools.partial(chain_kernel, n_tiles, tile_len, coupling),
+        out_shape=jax.ShapeDtypeStruct(square, F32),
+        in_specs=[smem, smem, vmem, vmem],
+        out_specs=vmem,
+        scratch_shapes=[pltpu.VMEM((total_slices, matrix_order), F32)],
+        compiler_params=pltpu.CompilerParams(vmem_limit_bytes=24 * 2**20),
+        cost_estimate=pl.CostEstimate(flops=3 * 10**10, bytes_accessed=4 * 10**6, transcendentals=0),
+        name="chain",
+    )(cols_of_tiles, where, field, weights)
     rows, guess, p_high, p_low = pl.pallas_call(
-        functools.partial(green_kernel, *sizes, coupling),
+        functools.partial(green_kernel, *sizes),
         out_shape=[jax.ShapeDtypeStruct((own_len, matrix_order), F32)] + [jax.ShapeDtypeStruct(square, BF16)] * 3,
-        in_specs=[smem, smem, vmem, vmem],
+        in_specs=[smem, smem, vmem],
         out_specs=[vmem] * 4,
-        scratch_shapes=[pltpu.VMEM((total_slices, matrix_order), F32), pltpu.VMEM(square, F32)] + [pltpu.VMEM(square, BF16)] * 3,
+        scratch_shapes=[pltpu.VMEM(square, BF16), pltpu.VMEM(square, F32)]
+        + [pltpu.VMEM(square, F8)] * 4,
         compiler_params=pltpu.CompilerParams(vmem_limit_bytes=32 * 2**20),
-        cost_estimate=pl.CostEstimate(flops=4 * 10**10, bytes_accessed=6 * 10**6, transcendentals=0),
+        cost_estimate=pl.CostEstimate(flops=5 * 10**9, bytes_accessed=6 * 10**6, transcendentals=0),
         name="green",
-    )(cols_of_tiles, where, field, weights)
+    )(cols_of_tiles, where, product)
     size = lax.axis_size("spin")
     other_rows = lax.ppermute(rows, "spin", [(i, (i + 1) % size) for i in range(size)])
     rest = pl.pallas_call(

time: 53.2 us -> 48.9 us (0.919)
  Pallas kernels: 44.1 us -> 41.9 us
  local copies, waits for them, and re-layouts: 2.13 us -> 0.01 us
    unnamed x10 -> x4, local copies, waits for them, and re-layouts: 2.13 us -> 0.01 us
    pallas_call x1 -> x2, Pallas kernels: 33.8 us -> 32.6 us  [the longest x1 26.7 us: per_device(): pl.pallas_call(functools.partial(chain_kernel, n_tiles, tile_len, couplin...]
    pallas_call x1, Pallas kernels: 5.97 us -> 4.93 us  [per_device(): pl.pallas_call(functools.partial(kinetic_kernel, n_tiles, tile_len, 0.5 /...]
  transfers between devices with their start and end apart: 4 -> 4, of which waited for: 1 -> 1; matrix products, arithmetic and copies ran while one was open for 0% -> 0% of each run, Pallas kernels for 16% -> 15%
where the time goes in v3:
time: 48.9 us; the launch traced here: 48.7 us
  Pallas kernels  41.9 us (86%)
  starting transfers between devices  6.16 us (13%)
    pallas_call x1, Pallas kernels, per_device(): pl.pallas_call(functools.partial(chain_kernel, n_tiles, tile_len, couplin...  26.7 us
    ppermute x3, starting transfers between devices, gather_blocks(): moved = lax.ppermute(packed, axis, pairs)  6.09 us
    pallas_call x1, Pallas kernels, per_device(): pl.pallas_call(functools.partial(green_kernel, *sizes), out_shape=[jax.Sh...  5.98 us
    pallas_call x1, Pallas kernels, per_device(): pl.pallas_call(functools.partial(kinetic_kernel, n_tiles, tile_len, 0.5 /...  4.93 us
    pallas_call x1, Pallas kernels, per_device(): pl.pallas_call(functools.partial(rest_kernel, *sizes), out_shape=jax.Shap...  2.38 us
    pallas_call x1, Pallas kernels, per_device(): pl.pallas_call(functools.partial(xcorr_kernel, *sizes), out_shape=jax.Sha...  1.94 us
  transfers between devices with their start and end apart: 4, of which 1 were waited for; matrix products, arithmetic and copies ran while one was open for 0% of the time, Pallas kernels for 15%

profile of v3, /device:TPU:0, one launch (start us, length us, event | category | flops | bytes accessed | tf_op | source)
XLA Modules:
  0.0 48.7 jit_solution(2934841902968272586)
XLA Ops:
  0.0 4.1 %collective-permute-start.1 = (s32[4,768]{1,0:T(4,128)}, s32[4,768]{1,0:T(4,128)S(1)}, u32[]{:S(2)}, u32[]{:S(2)}) collective-permute-start(s32[4,768]{1,0:T(4,128)} %param.4), channel_id=1, source_target_pairs={{8,0},{12,4},{0,8},{4,12},{9,1},{13,5},{1,9},{5,13},{10,2},{14,6},... | collective-permute-start | bytes 36872 | tf_op jit(solution)/shard_map/ppermute | solution.py:273
  4.1 1.3 %collective-permute-start = (s32[4,768]{1,0:T(4,128)}, s32[4,768]{1,0:T(4,128)S(1)}, u32[]{:S(2)}, u32[]{:S(2)}) collective-permute-start(s32[4,768]{1,0:T(4,128)} %param.4), channel_id=1, source_target_pairs={{4,0},{8,4},{12,8},{0,12},{5,1},{9,5},{13,9},{1,13},{6,2},{10,6},{... | collective-permute-start | bytes 36872 | tf_op jit(solution)/shard_map/ppermute | solution.py:273
  5.4 0.7 %collective-permute-start.2 = (s32[4,768]{1,0:T(4,128)}, s32[4,768]{1,0:T(4,128)S(1)}, u32[]{:S(2)}, u32[]{:S(2)}) collective-permute-start(s32[4,768]{1,0:T(4,128)} %param.4), channel_id=1, source_target_pairs={{12,0},{0,4},{4,8},{8,12},{13,1},{1,5},{5,9},{9,13},{14,2},{2,6},{... | collective-permute-start | bytes 36872 | tf_op jit(solution)/shard_map/ppermute | solution.py:273
  6.1 0.0 copy-start.1
  6.1 0.0 copy-start
  6.1 4.9 %kinetic.1.weight_ref = bf16[3,1024,256]{2,1,0:T(8,128)(2,1)S(1)} custom-call(s32[3,6]{1,0:T(4,128)} %bitcast.6, s32[2,3072]{1,0:T(2,128)} %bitcast.10, f32[1,3072]{1,0:T(1,128)} %bitcast.11), custom_call_target="tpu_custom_call" | custom-call | flops 4000000000 | bytes 4000000 | tf_op jit(solution)/shard_map/kinetic/pallas_call | solution.py:300
  11.0 0.1 pad_add_fusion.1.where_ref
  11.1 0.0 collective-permute-done.1
  11.1 0.0 collective-permute-done
  11.1 0.0 collective-permute-done.2
  11.1 0.0 copy-done.1
  11.2 0.0 copy-done
  11.2 26.7 %chain.1.z_ref = f32[768,768]{1,0:T(8,128)S(1)} custom-call(s32[3,6]{1,0:T(4,128)S(1)} %bitcast.7, s32[2]{0:T(128)S(1)} %pad_add_fusion.1.where_ref, s32[16,768]{1,0:T(8,128)S(1)} %pad_add_fusion.field_ref, bf16[3,1024,256]{2,1,0:T(8,128)(2,1)S(1)} %kinetic.1.weight_ref), custom_call_target="tpu_custom_call" | custom-call | flops 30000001024 | bytes 4000000 | tf_op jit(solution)/shard_map/chain/pallas_call | solution.py:319
  37.8 6.0 %green.1 = (f32[384,768]{1,0:T(8,128)S(1)}, bf16[768,768]{1,0:T(8,128)(2,1)S(1)}, bf16[768,768]{1,0:T(8,128)(2,1)S(1)}, bf16[768,768]{1,0:T(8,128)(2,1)S(1)}) custom-call(s32[3,6]{1,0:T(4,128)S(1)} %bitcast.8, s32[2]{0:T(128)S(1)} %pad_add_fusion.1.where_ref, f32[768,768]{1,0:T(8,128)S(1)} %chain.1.z_ref), custom_call_target="tpu_custom_call" | custom-call | flops 5000000000 | bytes 6000000 | tf_op jit(solution)/shard_map/green/pallas_call | solution.py:329
  43.8 0.1 collective-permute-start.3
  43.9 2.4 %rest.1.rest_ref = f32[384,384]{1,0:T(8,128)S(1)} custom-call(s32[3,6]{1,0:T(4,128)S(1)} %bitcast.9, s32[2]{0:T(128)S(1)} %pad_add_fusion.1.where_ref, bf16[768,768]{1,0:T(8,128)(2,1)S(1)} %get-tuple-element.10.guess_ref, bf16[768,768]{1,0:T(8,128)(2,1)S(1)} %get-tuple-element.11.p_high_ref, bf16[768,768]{1,0:T(8,128)(2,1)S(1)} %get-tuple-element.12.p_low_ref), custom_call_target="tpu_custom_call" | custom-call | flops 2000000000 | bytes 4000000 | tf_op jit(solution)/shard_map/rest/pallas_call | solution.py:342
  46.3 0.4 collective-permute-done.3.other_ref
  46.7 1.9 %xcorr.1 = f32[768,384]{1,0:T(8,128)} custom-call(s32[2]{0:T(128)S(1)} %pad_add_fusion.1.where_ref, f32[384,768]{1,0:T(8,128)S(1)} %get-tuple-element.9.rows_ref, f32[384,384]{1,0:T(8,128)S(1)} %rest.1.rest_ref, f32[384,768]{1,0:T(8,128)S(1)} %collective-permute-done.3.other_ref), custom_call_target="tpu_custom_call" | custom-call | tf_op jit(solution)/shard_map/xcorr/pallas_call | solution.py:352
  (1 shorter events, 0.0 us)
Async XLA Ops:
  0.0 11.1 %collective-permute-start.1 = (s32[4,768]{1,0:T(4,128)}, s32[4,768]{1,0:T(4,128)S(1)}, u32[]{:S(2)}, u32[]{:S(2)}) collective-permute-start(s32[4,768]{1,0:T(4,128)} %param.4), channel_id=1, source_target_pairs={{8,0},{12,4},{0,8},{4,12},{9,1},{13,5},{1,9},{5,13},{10,2},{14,6},... | collective-permute-start | bytes 36872 | tf_op jit(solution)/shard_map/ppermute | solution.py:273
  4.1 7.1 %collective-permute-start = (s32[4,768]{1,0:T(4,128)}, s32[4,768]{1,0:T(4,128)S(1)}, u32[]{:S(2)}, u32[]{:S(2)}) collective-permute-start(s32[4,768]{1,0:T(4,128)} %param.4), channel_id=1, source_target_pairs={{4,0},{8,4},{12,8},{0,12},{5,1},{9,5},{13,9},{1,13},{6,2},{10,6},{... | collective-permute-start | bytes 36872 | tf_op jit(solution)/shard_map/ppermute | solution.py:273
  5.4 5.7 %collective-permute-start.2 = (s32[4,768]{1,0:T(4,128)}, s32[4,768]{1,0:T(4,128)S(1)}, u32[]{:S(2)}, u32[]{:S(2)}) collective-permute-start(s32[4,768]{1,0:T(4,128)} %param.4), channel_id=1, source_target_pairs={{12,0},{0,4},{4,8},{8,12},{13,1},{1,5},{5,9},{9,13},{14,2},{2,6},{... | collective-permute-start | bytes 36872 | tf_op jit(solution)/shard_map/ppermute | solution.py:273
  6.1 5.0 %copy-start.1 = (s32[4,768]{1,0:T(4,128)S(1)}, s32[4,768]{1,0:T(4,128)}, u32[]{:S(2)}) copy-start(s32[4,768]{1,0:T(4,128)} %param.4) | copy-start | bytes 36868
  6.1 5.1 %copy-start = (s32[6,3]{0,1:T(4,128)S(1)}, s32[6,3]{0,1:T(4,128)}, u32[]{:S(2)}) copy-start(s32[6,3]{0,1:T(4,128)} %param.7) | copy-start | bytes 220
  43.8 2.9 %collective-permute-start.3 = (f32[384,768]{1,0:T(8,128)S(1)}, f32[384,768]{1,0:T(8,128)S(1)}, u32[]{:S(2)}, u32[]{:S(2)}) collective-permute-start(f32[384,768]{1,0:T(8,128)S(1)} %get-tuple-element.9.rows_ref), channel_id=1, source_target_pairs={{0,2},{2,0},{1,3},{3,1},{4,6},{6,4},{5,7},{7,5},{8,10},{10,8},{9,1... | collective-permute-start | bytes 3538952 | tf_op jit(solution)/shard_map/ppermute | solution.py:341

commit v4 on v3

--- a/solution.py
+++ b/solution.py
@@ -76,24 +76,25 @@
         weight = jnp.where(kept, hopping_ref[0:1, lanes] * scale, 0.0)
         weight_high = weight.astype(BF16).astype(F32)
         weight_low = weight - weight_high
-        swap = ((tile_a >> 1) != (tile_b >> 1)) & ((tile_a & 1) == 0)
+        together = (tile_a >> 1) == (tile_b >> 1)
+        swap = (tile_a != tile_b) & (together == ((tile_a & 1) == 1))
         first = jnp.where(swap, site_b, site_a)
         second = jnp.where(swap, site_a, site_b)
+        slot = jnp.where(together, first, second - (second & (tile_len - 1)) + tile_len + (first & (tile_len - 1)))
         row_ids = lax.broadcasted_iota(jnp.int32, (tile_len, chunk), 0)
         high_of, low_of, ones_of = [], [], []
         for p in range(n_tiles):
             ids = row_ids + p * tile_len
-            hit = first == ids
+            hit = slot == ids
             high_of.append(jnp.where(hit, weight_high, 0.0).astype(BF16))
             low_of.append(jnp.where(hit, weight_low, 0.0).astype(BF16))
             ones_of.append(jnp.where(second == ids, 1.0, 0.0).astype(BF16))
         for pair in range(n_tiles // 2):
-            tiles = [(2 * pair - 1) % n_tiles, 2 * pair, 2 * pair + 1]
+            tiles = [2 * pair, 2 * pair + 1]
             left = jnp.concatenate([high_of[t] for t in tiles] + [low_of[t] for t in tiles], axis=0)
             right = jnp.concatenate([ones_of[2 * pair], ones_of[2 * pair + 1]], axis=0)
             both = lax.dot_general(left, right, (((1,), (1,)), ((), ())), preferred_element_type=F32)
-            half = tile_len + pair_len
-            acc_ref[pair] += both[:half] + both[half:]
+            acc_ref[pair] += both[:pair_len] + both[pair_len:]
 
     for step in range(bonds // chunk):
         add_bonds(step)
@@ -101,12 +102,14 @@
     zero = jnp.zeros((tile_len, tile_len), BF16)
     n_pairs = n_tiles // 2
     for pair in range(n_pairs):
-        inner = acc_ref[pair, tile_len:, :]
+        lower = acc_ref[pair, tile_len:, :]
+        lower = jnp.concatenate([jnp.zeros((tile_len, tile_len), F32), lower[:, tile_len:]], axis=1)
+        inner = jnp.concatenate([acc_ref[pair, :tile_len, :], lower], axis=0)
         high, low = split(inner + inner.T + jnp.where(same, 1.0, 0.0))
         weight_ref[pair, :pair_len, :] = high
         weight_ref[pair, pair_len : 2 * pair_len, :] = low
-        above = acc_ref[pair, :tile_len, :tile_len]
-        below = acc_ref[(pair + 1) % n_pairs, :tile_len, :tile_len].T
+        above = acc_ref[pair, tile_len:, :tile_len]
+        below = acc_ref[(pair + 1) % n_pairs, tile_len:, :tile_len].T
         for side, cell in enumerate((above, below)):
             high, low = split(cell)
             base = (2 + side) * pair_len
@@ -140,34 +143,40 @@
         t = t % n_tiles
         return x[:, t * tile_len : (t + 1) * tile_len]
 
-    def one_slice(index):
+    def one_slice(index, reach):
         factor = factor_ref[pl.ds(index, 1), :]
-        for start in range(0, matrix_order, tile_len):
-            rows = slice(start, start + tile_len)
+        for p in range(n_tiles):
+            rows = slice(p * tile_len, (p + 1) * tile_len)
             high, low = split(z_ref[rows, :] * factor)
+
+            def live(t):
+                apart = (t - p) % n_tiles
+                return min(apart, n_tiles - apart) <= reach
+
             for pair in range(n_pairs):
                 lanes = slice(pair * pair_len, (pair + 1) * pair_len)
                 weight = weight_ref[pair]
-                inner = dot(
-                    jnp.concatenate([high[:, lanes], low[:, lanes], high[:, lanes]], axis=1),
-                    jnp.concatenate([weight[:pair_len], weight[:pair_len], weight[pair_len : 2 * pair_len]], axis=0),
-                )
+                inner = None
+                if live(2 * pair) or live(2 * pair + 1):
+                    inner = dot(
+                        jnp.concatenate([high[:, lanes], low[:, lanes], high[:, lanes]], axis=1),
+                        jnp.concatenate([weight[:pair_len], weight[:pair_len], weight[pair_len : 2 * pair_len]], axis=0),
+                    )
                 for side, t in enumerate((2 * pair - 1, 2 * pair + 2)):
-                    base = (2 + side) * pair_len
-                    part = dot(jnp.concatenate([tile(high, t), tile(low, t)], axis=1), weight[base : base + pair_len])
-                    at = slice(side * tile_len, (side + 1) * tile_len)
+                    parts = [] if inner is None else [inner[:, side * tile_len : (side + 1) * tile_len]]
+                    if live(t):
+                        base = (2 + side) * pair_len
+                        part = dot(jnp.concatenate([tile(high, t), tile(low, t)], axis=1), weight[base : base + pair_len])
+                        parts.append(part[:, :tile_len] + part[:, tile_len:])
                     to = (2 * pair + side) * tile_len
-                    z_ref[rows, to : to + tile_len] = inner[:, at] + (part[:, :tile_len] + part[:, tile_len:])
+                    z_ref[rows, to : to + tile_len] = sum(parts) if parts else jnp.zeros((tile_len, tile_len), F32)
 
     steps = slices - 1
-    together = 3 if steps % 3 == 0 else 1
-
-    def some_slices(step, carry):
-        for i in range(together):
-            one_slice(slices - 2 - step * together - i)
-        return carry
-
-    lax.fori_loop(0, steps // together, some_slices, 0)
+    peeled = steps if steps <= 16 else n_tiles // 2
+    for step in range(peeled):
+        one_slice(steps - 1 - step, step + 1)
+    if peeled < steps:
+        lax.fori_loop(peeled, steps, lambda step, carry: (one_slice(steps - 1 - step, n_tiles), carry)[1], 0)
 
 
 def corrected(places, tile_len, p_high_ref, p_low_ref, guess_ref):
@@ -303,7 +312,7 @@
         in_specs=[pl.BlockSpec(memory_space=pltpu.HBM)] * 3,
         out_specs=vmem,
         scratch_shapes=[
-            pltpu.VMEM((n_pairs, tile_len + pair_len, pair_len), F32),
+            pltpu.VMEM((n_pairs, pair_len, pair_len), F32),
             pltpu.SMEM(cols_of_tiles.shape, jnp.int32),
             pltpu.VMEM((2, hopping.shape[0]), jnp.int32),
             pltpu.VMEM((1, hopping.shape[0]), F32),

time: 48.9 us -> 47.1 us (0.963)
  Pallas kernels: 41.9 us -> 38.9 us
  waiting for transfers between devices: 0.45 us -> 1.64 us
    pallas_call x1, Pallas kernels: 26.7 us -> 24.9 us  [per_device(): pl.pallas_call(functools.partial(chain_kernel, n_tiles, tile_len, couplin...]
    pallas_call x1, Pallas kernels: 4.93 us -> 3.74 us  [per_device(): pl.pallas_call(functools.partial(kinetic_kernel, n_tiles, tile_len, 0.5 /...]
    ppermute x3, waiting for transfers between devices: 0.01 us -> 1.2 us  [gather_blocks(): moved = lax.ppermute(packed, axis, pairs)]
  transfers between devices with their start and end apart: 4 -> 4, of which waited for: 1 -> 2; matrix products, arithmetic and copies ran while one was open for 0% -> 0% of each run, Pallas kernels for 15% -> 13%
where the time goes in v4:
time: 47.1 us; the launch traced here: 46.9 us
  Pallas kernels  38.9 us (83%)
  starting transfers between devices  6.16 us (13%)
  waiting for transfers between devices  1.64 us (3%)
    pallas_call x1, Pallas kernels, per_device(): pl.pallas_call(functools.partial(chain_kernel, n_tiles, tile_len, couplin...  24.9 us
    ppermute x3, starting transfers between devices, gather_blocks(): moved = lax.ppermute(packed, axis, pairs)  6.09 us
    pallas_call x1, Pallas kernels, per_device(): pl.pallas_call(functools.partial(green_kernel, *sizes), out_shape=[jax.Sh...  5.98 us
    pallas_call x1, Pallas kernels, per_device(): pl.pallas_call(functools.partial(kinetic_kernel, n_tiles, tile_len, 0.5 /...  3.74 us
    pallas_call x1, Pallas kernels, per_device(): pl.pallas_call(functools.partial(rest_kernel, *sizes), out_shape=jax.Shap...  2.39 us
    pallas_call x1, Pallas kernels, per_device(): pl.pallas_call(functools.partial(xcorr_kernel, *sizes), out_shape=jax.Sha...  1.94 us
    ppermute x3, waiting for transfers between devices, gather_blocks(): moved = lax.ppermute(packed, axis, pairs)  1.2 us
  transfers between devices with their start and end apart: 4, of which 2 were waited for; matrix products, arithmetic and copies ran while one was open for 0% of the time, Pallas kernels for 13%

profile of v4, /device:TPU:0, one launch (start us, length us, event | category | flops | bytes accessed | tf_op | source)
XLA Modules:
  0.0 46.9 jit_solution(16279529499574117943)
XLA Ops:
  0.0 4.1 %collective-permute-start.1 = (s32[4,768]{1,0:T(4,128)}, s32[4,768]{1,0:T(4,128)S(1)}, u32[]{:S(2)}, u32[]{:S(2)}) collective-permute-start(s32[4,768]{1,0:T(4,128)} %param.4), channel_id=1, source_target_pairs={{8,0},{12,4},{0,8},{4,12},{9,1},{13,5},{1,9},{5,13},{10,2},{14,6},... | collective-permute-start | bytes 36872 | tf_op jit(solution)/shard_map/ppermute | solution.py:282
  4.1 1.3 %collective-permute-start = (s32[4,768]{1,0:T(4,128)}, s32[4,768]{1,0:T(4,128)S(1)}, u32[]{:S(2)}, u32[]{:S(2)}) collective-permute-start(s32[4,768]{1,0:T(4,128)} %param.4), channel_id=1, source_target_pairs={{4,0},{8,4},{12,8},{0,12},{5,1},{9,5},{13,9},{1,13},{6,2},{10,6},{... | collective-permute-start | bytes 36872 | tf_op jit(solution)/shard_map/ppermute | solution.py:282
  5.4 0.7 %collective-permute-start.2 = (s32[4,768]{1,0:T(4,128)}, s32[4,768]{1,0:T(4,128)S(1)}, u32[]{:S(2)}, u32[]{:S(2)}) collective-permute-start(s32[4,768]{1,0:T(4,128)} %param.4), channel_id=1, source_target_pairs={{12,0},{0,4},{4,8},{8,12},{13,1},{1,5},{5,9},{9,13},{14,2},{2,6},{... | collective-permute-start | bytes 36872 | tf_op jit(solution)/shard_map/ppermute | solution.py:282
  6.1 0.0 copy-start.1
  6.1 0.0 copy-start
  6.1 3.7 %kinetic.1.weight_ref = bf16[3,1024,256]{2,1,0:T(8,128)(2,1)S(1)} custom-call(s32[3,6]{1,0:T(4,128)} %bitcast.6, s32[2,3072]{1,0:T(2,128)} %bitcast.10, f32[1,3072]{1,0:T(1,128)} %bitcast.11), custom_call_target="tpu_custom_call" | custom-call | flops 4000000000 | bytes 4000000 | tf_op jit(solution)/shard_map/kinetic/pallas_call | solution.py:309
  9.8 0.1 pad_add_fusion.1.where_ref
  9.9 0.0 collective-permute-done.1
  9.9 0.0 collective-permute-done
  9.9 1.2 %collective-permute-done.2 = s32[4,768]{1,0:T(4,128)S(1)} collective-permute-done((s32[4,768]{1,0:T(4,128)}, s32[4,768]{1,0:T(4,128)S(1)}, u32[]{:S(2)}, u32[]{:S(2)}) %collective-permute-start.2) | collective-permute-done | bytes 12320 | tf_op jit(solution)/shard_map/ppermute | solution.py:282
  11.1 0.0 copy-done.1
  11.1 0.0 copy-done
  11.2 24.9 %chain.1.z_ref = f32[768,768]{1,0:T(8,128)S(1)} custom-call(s32[3,6]{1,0:T(4,128)S(1)} %bitcast.7, s32[2]{0:T(128)S(1)} %pad_add_fusion.1.where_ref, s32[16,768]{1,0:T(8,128)S(1)} %pad_add_fusion.field_ref, bf16[3,1024,256]{2,1,0:T(8,128)(2,1)S(1)} %kinetic.1.weight_ref), custom_call_target="tpu_custom_call" | custom-call | flops 30000001024 | bytes 4000000 | tf_op jit(solution)/shard_map/chain/pallas_call | solution.py:328
  36.0 6.0 %green.1 = (f32[384,768]{1,0:T(8,128)S(1)}, bf16[768,768]{1,0:T(8,128)(2,1)S(1)}, bf16[768,768]{1,0:T(8,128)(2,1)S(1)}, bf16[768,768]{1,0:T(8,128)(2,1)S(1)}) custom-call(s32[3,6]{1,0:T(4,128)S(1)} %bitcast.8, s32[2]{0:T(128)S(1)} %pad_add_fusion.1.where_ref, f32[768,768]{1,0:T(8,128)S(1)} %chain.1.z_ref), custom_call_target="tpu_custom_call" | custom-call | flops 5000000000 | bytes 6000000 | tf_op jit(solution)/shard_map/green/pallas_call | solution.py:338
  42.0 0.1 collective-permute-start.3
  42.1 2.4 %rest.1.rest_ref = f32[384,384]{1,0:T(8,128)S(1)} custom-call(s32[3,6]{1,0:T(4,128)S(1)} %bitcast.9, s32[2]{0:T(128)S(1)} %pad_add_fusion.1.where_ref, bf16[768,768]{1,0:T(8,128)(2,1)S(1)} %get-tuple-element.10.guess_ref, bf16[768,768]{1,0:T(8,128)(2,1)S(1)} %get-tuple-element.11.p_high_ref, bf16[768,768]{1,0:T(8,128)(2,1)S(1)} %get-tuple-element.12.p_low_ref), custom_call_target="tpu_custom_call" | custom-call | flops 2000000000 | bytes 4000000 | tf_op jit(solution)/shard_map/rest/pallas_call | solution.py:351
  44.5 0.4 collective-permute-done.3.other_ref
  44.9 1.9 %xcorr.1 = f32[768,384]{1,0:T(8,128)} custom-call(s32[2]{0:T(128)S(1)} %pad_add_fusion.1.where_ref, f32[384,768]{1,0:T(8,128)S(1)} %get-tuple-element.9.rows_ref, f32[384,384]{1,0:T(8,128)S(1)} %rest.1.rest_ref, f32[384,768]{1,0:T(8,128)S(1)} %collective-permute-done.3.other_ref), custom_call_target="tpu_custom_call" | custom-call | tf_op jit(solution)/shard_map/xcorr/pallas_call | solution.py:361
  (1 shorter events, 0.0 us)
Async XLA Ops:
  0.0 9.9 %collective-permute-start.1 = (s32[4,768]{1,0:T(4,128)}, s32[4,768]{1,0:T(4,128)S(1)}, u32[]{:S(2)}, u32[]{:S(2)}) collective-permute-start(s32[4,768]{1,0:T(4,128)} %param.4), channel_id=1, source_target_pairs={{8,0},{12,4},{0,8},{4,12},{9,1},{13,5},{1,9},{5,13},{10,2},{14,6},... | collective-permute-start | bytes 36872 | tf_op jit(solution)/shard_map/ppermute | solution.py:282
  4.1 5.9 %collective-permute-start = (s32[4,768]{1,0:T(4,128)}, s32[4,768]{1,0:T(4,128)S(1)}, u32[]{:S(2)}, u32[]{:S(2)}) collective-permute-start(s32[4,768]{1,0:T(4,128)} %param.4), channel_id=1, source_target_pairs={{4,0},{8,4},{12,8},{0,12},{5,1},{9,5},{13,9},{1,13},{6,2},{10,6},{... | collective-permute-start | bytes 36872 | tf_op jit(solution)/shard_map/ppermute | solution.py:282
  5.4 5.7 %collective-permute-start.2 = (s32[4,768]{1,0:T(4,128)}, s32[4,768]{1,0:T(4,128)S(1)}, u32[]{:S(2)}, u32[]{:S(2)}) collective-permute-start(s32[4,768]{1,0:T(4,128)} %param.4), channel_id=1, source_target_pairs={{12,0},{0,4},{4,8},{8,12},{13,1},{1,5},{5,9},{9,13},{14,2},{2,6},{... | collective-permute-start | bytes 36872 | tf_op jit(solution)/shard_map/ppermute | solution.py:282
  6.1 5.0 %copy-start.1 = (s32[4,768]{1,0:T(4,128)S(1)}, s32[4,768]{1,0:T(4,128)}, u32[]{:S(2)}) copy-start(s32[4,768]{1,0:T(4,128)} %param.4) | copy-start | bytes 36868
  6.1 5.0 %copy-start = (s32[6,3]{0,1:T(4,128)S(1)}, s32[6,3]{0,1:T(4,128)}, u32[]{:S(2)}) copy-start(s32[6,3]{0,1:T(4,128)} %param.7) | copy-start | bytes 220
  42.0 2.9 %collective-permute-start.3 = (f32[384,768]{1,0:T(8,128)S(1)}, f32[384,768]{1,0:T(8,128)S(1)}, u32[]{:S(2)}, u32[]{:S(2)}) collective-permute-start(f32[384,768]{1,0:T(8,128)S(1)} %get-tuple-element.9.rows_ref), channel_id=1, source_target_pairs={{0,2},{2,0},{1,3},{3,1},{4,6},{6,4},{5,7},{7,5},{8,10},{10,8},{9,1... | collective-permute-start | bytes 3538952 | tf_op jit(solution)/shard_map/ppermute | solution.py:350

commit v5 on v4

--- a/solution.py
+++ b/solution.py
@@ -117,41 +117,43 @@
             weight_ref[pair, base + tile_len : base + pair_len, :] = jnp.concatenate([high, zero], axis=1)
 
 
-def chain(n_tiles, tile_len, factor_ref, weight_ref, z_ref):
+def chain(n_tiles, tile_len, parity, factor_ref, weight_ref, targets):
     slices, matrix_order = factor_ref.shape
     n_pairs = n_tiles // 2
     pair_len = 2 * tile_len
 
-    for p in range(n_tiles):
+    def first_rows(p):
         row = factor_ref[slices - 1 : slices, p * tile_len : (p + 1) * tile_len]
         column = jnp.broadcast_to(row, (tile_len, tile_len)).T
-        rows = slice(p * tile_len, (p + 1) * tile_len)
-        z_ref[rows, :] = jnp.zeros((tile_len, matrix_order), F32)
         own = p // 2
         at = (p % 2) * tile_len
         whole = weight_ref[own, at : at + tile_len, :].astype(F32) + weight_ref[own, pair_len + at : pair_len + at + tile_len, :].astype(F32)
-        z_ref[rows, own * pair_len : (own + 1) * pair_len] = jnp.concatenate([column, column], axis=1) * whole
         if p % 2:
-            into, base, to = (own + 1) % n_pairs, 2 * pair_len, 0
+            into, base, next_tile = (own + 1) % n_pairs, 2 * pair_len, (p + 1) % n_tiles
         else:
-            into, base, to = (own - 1) % n_pairs, 3 * pair_len, tile_len
+            into, base, next_tile = (own - 1) % n_pairs, 3 * pair_len, (p - 1) % n_tiles
         cell = weight_ref[into, base : base + tile_len, :].astype(F32)
-        to = into * pair_len + to
-        z_ref[rows, to : to + tile_len] = column * (cell[:, :tile_len] + cell[:, tile_len:])
+        cells = [jnp.zeros((tile_len, tile_len), F32)] * n_tiles
+        cells[2 * own] = column * whole[:, :tile_len]
+        cells[2 * own + 1] = column * whole[:, tile_len:]
+        cells[next_tile] = column * (cell[:, :tile_len] + cell[:, tile_len:])
+        return jnp.concatenate(cells, axis=1)
+
+    started = targets[0][1] is not None
+    for z_ref, _, rows, tiles in [] if started else targets:
+        z_ref[rows, :] = first_rows(tiles[0]) if len(tiles) == 1 else jnp.where(parity == 0, first_rows(tiles[0]), first_rows(tiles[1]))
 
     def tile(x, t):
         t = t % n_tiles
         return x[:, t * tile_len : (t + 1) * tile_len]
 
-    def one_slice(index, reach):
+    def one_slice(index, reach, afresh=False):
         factor = factor_ref[pl.ds(index, 1), :]
-        for p in range(n_tiles):
-            rows = slice(p * tile_len, (p + 1) * tile_len)
-            high, low = split(z_ref[rows, :] * factor)
+        for z_ref, source_ref, rows, tiles in targets:
+            high, low = split((source_ref if afresh else z_ref)[rows, :] * factor)
 
             def live(t):
-                apart = (t - p) % n_tiles
-                return min(apart, n_tiles - apart) <= reach
+                return any(min((t - p) % n_tiles, (p - t) % n_tiles) <= reach for p in tiles)
 
             for pair in range(n_pairs):
                 lanes = slice(pair * pair_len, (pair + 1) * pair_len)
@@ -171,10 +173,10 @@
                     to = (2 * pair + side) * tile_len
                     z_ref[rows, to : to + tile_len] = sum(parts) if parts else jnp.zeros((tile_len, tile_len), F32)
 
-    steps = slices - 1
+    steps = slices if started else slices - 1
     peeled = steps if steps <= 16 else n_tiles // 2
     for step in range(peeled):
-        one_slice(steps - 1 - step, step + 1)
+        one_slice(steps - 1 - step, n_tiles if started else step + 1, started and step == 0)
     if peeled < steps:
         lax.fori_loop(peeled, steps, lambda step, carry: (one_slice(steps - 1 - step, n_tiles), carry)[1], 0)
 
@@ -197,27 +199,39 @@
     return own, rest
 
 
-def chain_kernel(n_tiles, tile_len, coupling, tile_cols_ref, where_ref, field_ref, weight_ref, z_ref, factor_ref):
+def chain_kernel(n_tiles, tile_len, coupling, tiles_of, tile_cols_ref, where_ref, field_ref, weight_ref, *refs):
+    *z_refs, factor_ref = refs
+    parts = len(tiles_of)
+    sources, z_refs = (z_refs[:-parts] or [None] * parts), z_refs[-parts:]
     order = cycle_order(tile_cols_ref, n_tiles)
     sign = 1.0 - 2.0 * where_ref[0].astype(F32)
     for p in range(n_tiles):
         spins_pm = (2 * field_ref[:, tile_ds(order[p], tile_len)] - 1).astype(F32)
         factor_ref[:, p * tile_len : (p + 1) * tile_len] = jnp.exp(sign * coupling * spins_pm)
-    chain(n_tiles, tile_len, factor_ref, weight_ref, z_ref)
+    targets = []
+    for z_ref, source_ref, tiles_in in zip(z_refs, sources, tiles_of):
+        targets += [(z_ref, source_ref, slice(i * tile_len, (i + 1) * tile_len), tiles) for i, tiles in enumerate(tiles_in)]
+    chain(n_tiles, tile_len, where_ref[2], factor_ref, weight_ref, targets)
 
 
 def green_kernel(
-    n_tiles, tile_len, own_tiles, tile_cols_ref, where_ref, z_ref,
+    n_tiles, tile_len, own_tiles, tile_cols_ref, where_ref, mine_ref, theirs_ref, common_ref, last_ref,
     rows_ref, guess_ref, p_high_ref, p_low_ref, b_ref, c_ref, one8_ref, two8_ref, part8_ref, four8_ref,
 ):
     order = cycle_order(tile_cols_ref, n_tiles)
-    matrix_order = z_ref.shape[1]
+    matrix_order = mine_ref.shape[1]
     block = 2 * tile_len
     blocks = [slice(start, start + block) for start in range(0, matrix_order, block)]
-    col_max = jnp.max(jnp.sum(z_ref[...], axis=0, keepdims=True), axis=1, keepdims=True)
-    shrink = 0.5 / col_max
-    for rows in blocks:
-        p_rows = z_ref[rows, :] * shrink
+    even = where_ref[2] == 0
+    first, second = mine_ref[...], theirs_ref[...]
+    pieces = [jnp.where(even, first, second), jnp.where(even, second, first)]
+    for z_ref in (common_ref, last_ref):
+        pieces += [z_ref[start : start + tile_len, :] for start in range(0, z_ref.shape[0], tile_len)]
+    col_sum = sum(jnp.sum(piece, axis=0, keepdims=True) for piece in pieces)
+    shrink = 0.5 / jnp.max(col_sum, axis=1, keepdims=True)
+    for p, piece in enumerate(pieces):
+        rows = slice(p * tile_len, (p + 1) * tile_len)
+        p_rows = piece * shrink
         p_high_ref[rows, :], p_low_ref[rows, :] = split(p_rows)
         one8_ref[rows, :] = (p_rows * 2.0**9).astype(F8)
     for rows in blocks:
@@ -249,42 +263,40 @@
         out_ref[:, i * tile_len : (i + 1) * tile_len] = y_ref[:, tile_ds(place_of(order, t), tile_len)]
 
 
-def xcorr_kernel(n_tiles, tile_len, own_tiles, where_ref, rows_ref, rest_ref, other_ref, out_ref):
+def xcorr_kernel(n_tiles, tile_len, own_tiles, where_ref, rows_ref, rest_ref, other_ref, out_ref, block_ref, sems):
     own, rest = tiles_of_rows(where_ref, n_tiles, own_tiles)
-    width = own_tiles * tile_len
-    for i, t in enumerate(own):
-        rows = slice(i * tile_len, (i + 1) * tile_len)
-        for j, u in enumerate(own):
-            cols = slice(j * tile_len, (j + 1) * tile_len)
-            green = -rows_ref[rows, tile_ds(u, tile_len)]
-            if i == j:
-                ids = (tile_len, tile_len)
-                green += jnp.where(lax.broadcasted_iota(jnp.int32, ids, 0) == lax.broadcasted_iota(jnp.int32, ids, 1), 1.0, 0.0)
-            out_ref[tile_ds(t, tile_len), cols] = green * other_ref[cols, tile_ds(t, tile_len)].T
-    for i, t in enumerate(rest):
-        rows = slice(i * tile_len, (i + 1) * tile_len)
+    ids = (tile_len, tile_len)
+    one = jnp.where(lax.broadcasted_iota(jnp.int32, ids, 0) == lax.broadcasted_iota(jnp.int32, ids, 1), 1.0, 0.0)
+    copies = []
+    for i, t in enumerate(own + rest):
         for j in range(own_tiles):
             cols = slice(j * tile_len, (j + 1) * tile_len)
-            out_ref[tile_ds(t, tile_len), cols] = -rest_ref[rows, cols] * other_ref[cols, tile_ds(t, tile_len)].T
+            if i < own_tiles:
+                green = -rows_ref[i * tile_len : (i + 1) * tile_len, tile_ds(own[j], tile_len)]
+                if i == j:
+                    green += one
+            else:
+                green = -rest_ref[(i - own_tiles) * tile_len : (i - own_tiles + 1) * tile_len, cols]
+            block_ref[i, :, cols] = green * other_ref[cols, tile_ds(t, tile_len)].T
+        copies.append(pltpu.make_async_copy(block_ref.at[i], out_ref.at[tile_ds(t, tile_len), :], sems.at[i]))
+        copies[-1].start()
+    for copy in copies:
+        copy.wait()
+
+
+def from_ahead(x, axis, by):
+    size = lax.axis_size(axis)
+    return lax.ppermute(x, axis, [((i + by) % size, i) for i in range(size)])
 
 
 def gather_blocks(field, axis):
     size = lax.axis_size(axis)
-    held, count = [field], 1
-    while count < size:
-        grown = list(held)
-        for step in range(1, 4):
-            by = step * count
-            if by >= size:
-                break
-            pairs = [((i + by) % size, i) for i in range(size)]
-            packed = held[0] if len(held) == 1 else jnp.concatenate(held, axis=0)
-            moved = lax.ppermute(packed, axis, pairs)
-            grown.append(moved)
-        held = grown
-        count = min(size, count * 4)
-        held = [jnp.concatenate(held, axis=0)]
-    return held[0]
+    behind = from_ahead(field, axis, -1)
+    held, by = jnp.concatenate([behind, field], axis=0), 2
+    while by < size:
+        held = jnp.concatenate([held, from_ahead(held, axis, by)], axis=0)
+        by *= 2
+    return behind, held[field.shape[0] :]
 
 
 def per_device(ising_field, bond_sites, hopping, tile_cols):
@@ -304,7 +316,7 @@
     coupling = 1.5 / math.sqrt(total_slices)
     smem = pl.BlockSpec(memory_space=pltpu.SMEM)
     vmem = pl.BlockSpec(memory_space=pltpu.VMEM)
-    field = gather_blocks(ising_field, "tm")
+    behind, ahead = gather_blocks(ising_field, "tm")
     cols_of_tiles = tile_cols.T
     weights = pl.pallas_call(
         functools.partial(kinetic_kernel, n_tiles, tile_len, 0.5 / total_slices),
@@ -322,30 +334,40 @@
         cost_estimate=pl.CostEstimate(flops=4 * 10**9, bytes_accessed=4 * 10**6, transcendentals=0),
         name="kinetic",
     )(*[pltpu.with_memory_space_constraint(x, pltpu.HBM) for x in (cols_of_tiles, bond_sites.T, hopping[None, :])])
-    where = jnp.stack([lax.axis_index("spin"), lax.axis_index("rows") // shared]).astype(jnp.int32)
+    where = jnp.stack([lax.axis_index("spin"), lax.axis_index("rows") // shared, lax.axis_index("rows") % 2]).astype(jnp.int32)
     square = (matrix_order, matrix_order)
     sizes = (n_tiles, tile_len, own_tiles)
-    product = pl.pallas_call(
-        functools.partial(chain_kernel, n_tiles, tile_len, coupling),
-        out_shape=jax.ShapeDtypeStruct(square, F32),
-        in_specs=[smem, smem, vmem, vmem],
-        out_specs=vmem,
-        scratch_shapes=[pltpu.VMEM((total_slices, matrix_order), F32)],
-        compiler_params=pltpu.CompilerParams(vmem_limit_bytes=24 * 2**20),
-        cost_estimate=pl.CostEstimate(flops=3 * 10**10, bytes_accessed=4 * 10**6, transcendentals=0),
-        name="chain",
-    )(cols_of_tiles, where, field, weights)
+
+    def chain_part(field, sources, *tiles_of):
+        lengths = [len(tiles) * tile_len for tiles in tiles_of]
+        return pl.pallas_call(
+            functools.partial(chain_kernel, n_tiles, tile_len, coupling, tiles_of),
+            out_shape=[jax.ShapeDtypeStruct((length, matrix_order), F32) for length in lengths],
+            in_specs=[smem, smem] + [vmem] * (2 + len(sources)),
+            out_specs=[vmem] * len(lengths),
+            scratch_shapes=[pltpu.VMEM((field.shape[0], matrix_order), F32)],
+            compiler_params=pltpu.CompilerParams(vmem_limit_bytes=24 * 2**20),
+            cost_estimate=pl.CostEstimate(flops=25 * 10**5 * sum(lengths) * field.shape[0], bytes_accessed=4 * 10**6, transcendentals=0),
+            name="chain",
+        )(cols_of_tiles, where, field, weights, *sources)
+
+    half = n_tiles // 2
+    shared_tile, common_tiles, last_tiles = [(0, 1)], [(p,) for p in range(2, half)], [(p,) for p in range(half, n_tiles)]
+    mine, common, last = chain_part(behind, [], shared_tile, common_tiles, last_tiles)
+    mine, common = chain_part(ahead, [mine, common], shared_tile, common_tiles)
+    theirs = lax.ppermute(mine, "rows", [(i, i ^ 1) for i in range(n_rows)])
+    (last,) = chain_part(ahead, [last], last_tiles)
     rows, guess, p_high, p_low = pl.pallas_call(
         functools.partial(green_kernel, *sizes),
         out_shape=[jax.ShapeDtypeStruct((own_len, matrix_order), F32)] + [jax.ShapeDtypeStruct(square, BF16)] * 3,
-        in_specs=[smem, smem, vmem],
+        in_specs=[smem, smem] + [vmem] * 4,
         out_specs=[vmem] * 4,
         scratch_shapes=[pltpu.VMEM(square, BF16), pltpu.VMEM(square, F32)]
         + [pltpu.VMEM(square, F8)] * 4,
         compiler_params=pltpu.CompilerParams(vmem_limit_bytes=32 * 2**20),
         cost_estimate=pl.CostEstimate(flops=5 * 10**9, bytes_accessed=6 * 10**6, transcendentals=0),
         name="green",
-    )(cols_of_tiles, where, product)
+    )(cols_of_tiles, where, mine, theirs, common, last)
     size = lax.axis_size("spin")
     other_rows = lax.ppermute(rows, "spin", [(i, (i + 1) % size) for i in range(size)])
     rest = pl.pallas_call(
@@ -362,7 +384,8 @@
         functools.partial(xcorr_kernel, *sizes),
         out_shape=jax.ShapeDtypeStruct((matrix_order, own_len), F32),
         in_specs=[smem, vmem, vmem, vmem],
-        out_specs=vmem,
+        out_specs=pl.BlockSpec(memory_space=pltpu.HBM),
+        scratch_shapes=[pltpu.VMEM((n_tiles, tile_len, own_len), F32), pltpu.SemaphoreType.DMA((n_tiles,))],
         compiler_params=pltpu.CompilerParams(vmem_limit_bytes=16 * 2**20),
         name="xcorr",
     )(where, rows, rest, other_rows)

time: 47.1 us -> 45.9 us (0.975)
  Pallas kernels: 38.9 us -> 37.6 us
  waiting for transfers between devices: 1.64 us -> 0.53 us
  starting transfers between devices: 6.16 us -> 7.25 us
    pallas_call x1 -> x3, Pallas kernels: 24.9 us -> 23.3 us  [chain_part(): pl.pallas_call(functools.partial(chain_kernel, n_tiles, tile_len, couplin...]
    ppermute x3, waiting for transfers between devices: 1.2 us -> 0.09 us  [the longest x2 0.08 us: from_ahead(): return lax.ppermute(x, axis, [((i + by) % size, i) for i in range(size)])]
    ppermute x3, starting transfers between devices: 6.09 us -> 7.18 us  [the longest x2 5.63 us: from_ahead(): return lax.ppermute(x, axis, [((i + by) % size, i) for i in range(size)])]
  transfers between devices with their start and end apart: 4 -> 4, of which waited for: 2 -> 2; matrix products, arithmetic and copies ran while one was open for 0% -> 0% of each run, Pallas kernels for 13% -> 47%
where the time goes in v5:
time: 45.9 us; the launch traced here: 45.8 us
  Pallas kernels  37.6 us (82%)
  starting transfers between devices  7.25 us (16%)
  waiting for transfers between devices  0.53 us (1%)
    pallas_call x3, Pallas kernels, chain_part(): pl.pallas_call(functools.partial(chain_kernel, n_tiles, tile_len, couplin...  23.3 us
    pallas_call x1, Pallas kernels, per_device(): pl.pallas_call(functools.partial(green_kernel, *sizes), out_shape=[jax.Sh...  6.42 us
    ppermute x2, starting transfers between devices, from_ahead(): return lax.ppermute(x, axis, [((i + by) % size, i) for i in range(size)])  5.63 us
    pallas_call x1, Pallas kernels, per_device(): pl.pallas_call(functools.partial(kinetic_kernel, n_tiles, tile_len, 0.5 /...  3.74 us
    pallas_call x1, Pallas kernels, per_device(): pl.pallas_call(functools.partial(rest_kernel, *sizes), out_shape=jax.Shap...  2.38 us
    pallas_call x1, Pallas kernels, per_device(): pl.pallas_call(functools.partial(xcorr_kernel, *sizes), out_shape=jax.Sha...  1.73 us
    ppermute x1, starting transfers between devices, per_device(): theirs = lax.ppermute(mine, 'rows', [(i, i ^ 1) for i in range(n_rows)])  1.55 us
  transfers between devices with their start and end apart: 4, of which 2 were waited for; matrix products, arithmetic and copies ran while one was open for 0% of the time, Pallas kernels for 47%

profile of v5, /device:TPU:0, one launch (start us, length us, event | category | flops | bytes accessed | tf_op | source)
XLA Modules:
  0.0 45.8 jit_solution(4974204735685871097)
XLA Ops:
  0.0 3.1 %collective-permute-start = (s32[4,768]{1,0:T(4,128)}, s32[4,768]{1,0:T(4,128)S(1)}, u32[]{:S(2)}, u32[]{:S(2)}) collective-permute-start(s32[4,768]{1,0:T(4,128)} %param.4), channel_id=1, source_target_pairs={{12,0},{0,4},{4,8},{8,12},{13,1},{1,5},{5,9},{9,13},{14,2},{2,6},{... | collective-permute-start | bytes 36872 | tf_op jit(solution)/shard_map/ppermute | solution.py:289
  3.1 0.0 copy-start.1
  3.1 0.0 copy-start
  3.1 3.7 %kinetic.1.weight_ref = bf16[3,1024,256]{2,1,0:T(8,128)(2,1)S(1)} custom-call(s32[3,6]{1,0:T(4,128)} %bitcast.7, s32[2,3072]{1,0:T(2,128)} %bitcast.13, f32[1,3072]{1,0:T(1,128)} %bitcast.14), custom_call_target="tpu_custom_call" | custom-call | flops 4000000000 | bytes 4000000 | tf_op jit(solution)/shard_map/kinetic/pallas_call | solution.py:321
  6.8 0.1 pad_add_fusion.2.where_ref
  6.9 0.1 collective-permute-done.field_ref
  7.0 0.0 copy-done.1
  7.0 2.6 %collective-permute-start.1 = (s32[8,768]{1,0:T(8,128)S(1)}, s32[8,768]{1,0:T(8,128)S(1)}, u32[]{:S(2)}, u32[]{:S(2)}) collective-permute-start(s32[8,768]{1,0:T(8,128)S(1)} %pad_add_fusion.1), channel_id=1, source_target_pairs={{8,0},{12,4},{0,8},{4,12},{9,1},{13,5},{1,9},{5,13},{10,2},{14,6},... | collective-permute-start | bytes 73736 | tf_op jit(solution)/shard_map/ppermute | solution.py:289
  9.6 0.0 copy-done
  9.6 4.6 %chain.3 = (f32[128,768]{1,0:T(8,128)S(1)}, f32[128,768]{1,0:T(8,128)S(1)}, f32[384,768]{1,0:T(8,128)S(1)}) custom-call(s32[3,6]{1,0:T(4,128)S(1)} %bitcast.8, s32[3]{0:T(128)S(1)} %pad_add_fusion.2.where_ref, s32[4,768]{1,0:T(4,128)S(1)} %collective-permute-done.field_ref, bf16[3,1024,256]{2,1,0:T(8,128)(2,1)S(1)} %kinetic.1.weight_ref), custom_call_target="tpu_custom_call" | custom-call | flops 6400000000 | bytes 4000000 | tf_op jit(solution)/shard_map/chain/pallas_call | solution.py:343
  14.1 0.0 collective-permute-done.1
  14.2 7.8 %chain.4 = (f32[128,768]{1,0:T(8,128)S(1)}, f32[128,768]{1,0:T(8,128)S(1)}) custom-call(s32[3,6]{1,0:T(4,128)S(1)} %bitcast.9, s32[3]{0:T(128)S(1)} %pad_add_fusion.2.where_ref, s32[12,768]{1,0:T(8,128)S(1)} %pad_add_fusion.field_ref, bf16[3,1024,256]{2,1,0:T(8,128)(2,1)S(1)} %kinetic.1.weight_ref, f32[128,768]{1,0:T(8,128)S(1)} %get-tuple-element.14.refs_0_, ...), custom_call_target="tpu_custom_call" | custom-call | flops 7680000000 | bytes 4000000 | tf_op jit(solution)/shard_map/chain/pallas_call | solution.py:343
  22.0 1.5 %collective-permute-start.2 = (f32[128,768]{1,0:T(8,128)S(1)}, f32[128,768]{1,0:T(8,128)S(1)}, u32[]{:S(2)}, u32[]{:S(2)}) collective-permute-start(f32[128,768]{1,0:T(8,128)S(1)} %get-tuple-element.16.mine_ref), channel_id=1, source_target_pairs={{0,1},{1,0},{2,3},{3,2},{4,5},{5,4},{6,7},{7,6},{8,9},{9,8},{10,11... | collective-permute-start | bytes 1179656 | tf_op jit(solution)/shard_map/ppermute | solution.py:358
  23.6 10.9 %chain.5.last_ref = f32[384,768]{1,0:T(8,128)S(1)} custom-call(s32[3,6]{1,0:T(4,128)S(1)} %bitcast.10, s32[3]{0:T(128)S(1)} %pad_add_fusion.2.where_ref, s32[12,768]{1,0:T(8,128)S(1)} %pad_add_fusion.field_ref, bf16[3,1024,256]{2,1,0:T(8,128)(2,1)S(1)} %kinetic.1.weight_ref, f32[384,768]{1,0:T(8,128)S(1)} %get-tuple-element.18.refs_0_), custom_call_target="tpu_custom_call" | custom-call | flops 11520000000 | bytes 4000000 | tf_op jit(solution)/shard_map/chain/pallas_call | solution.py:343
  34.5 0.0 collective-permute-done.2.theirs_ref
  34.5 6.4 %green.1 = (f32[384,768]{1,0:T(8,128)S(1)}, bf16[768,768]{1,0:T(8,128)(2,1)S(1)}, bf16[768,768]{1,0:T(8,128)(2,1)S(1)}, bf16[768,768]{1,0:T(8,128)(2,1)S(1)}) custom-call(s32[3,6]{1,0:T(4,128)S(1)} %bitcast.11, s32[3]{0:T(128)S(1)} %pad_add_fusion.2.where_ref, f32[128,768]{1,0:T(8,128)S(1)} %get-tuple-element.16.mine_ref, ...), custom_call_target="tpu_custom_call" | custom-call | flops 5000000000 | bytes 6000000 | tf_op jit(solution)/shard_map/green/pallas_call | solution.py:360
  40.9 0.1 collective-permute-start.3
  41.0 2.4 %rest.1.rest_ref = f32[384,384]{1,0:T(8,128)S(1)} custom-call(s32[3,6]{1,0:T(4,128)S(1)} %bitcast.12, s32[3]{0:T(128)S(1)} %pad_add_fusion.2.where_ref, bf16[768,768]{1,0:T(8,128)(2,1)S(1)} %get-tuple-element.20.guess_ref, bf16[768,768]{1,0:T(8,128)(2,1)S(1)} %get-tuple-element.21.p_high_ref, bf16[768,768]{1,0:T(8,128)(2,1)S(1)} %get-tuple-element.22.p_low_ref), custom_call_target="tpu_custom_call" | custom-call | flops 2000000000 | bytes 4000000 | tf_op jit(solution)/shard_map/rest/pallas_call | solution.py:373
  43.4 0.4 collective-permute-done.3.other_ref
  43.9 1.7 %xcorr.1 = f32[768,384]{1,0:T(8,128)} custom-call(s32[3]{0:T(128)S(1)} %pad_add_fusion.2.where_ref, f32[384,768]{1,0:T(8,128)S(1)} %get-tuple-element.19.rows_ref, f32[384,384]{1,0:T(8,128)S(1)} %rest.1.rest_ref, f32[384,768]{1,0:T(8,128)S(1)} %collective-permute-done.3.other_ref), custom_call_target="tpu_custom_call" | custom-call | tf_op jit(solution)/shard_map/xcorr/pallas_call | solution.py:383
  (2 shorter events, 0.0 us)
Async XLA Ops:
  0.0 7.0 %collective-permute-start = (s32[4,768]{1,0:T(4,128)}, s32[4,768]{1,0:T(4,128)S(1)}, u32[]{:S(2)}, u32[]{:S(2)}) collective-permute-start(s32[4,768]{1,0:T(4,128)} %param.4), channel_id=1, source_target_pairs={{12,0},{0,4},{4,8},{8,12},{13,1},{1,5},{5,9},{9,13},{14,2},{2,6},{... | collective-permute-start | bytes 36872 | tf_op jit(solution)/shard_map/ppermute | solution.py:289
  3.1 3.9 %copy-start.1 = (s32[4,768]{1,0:T(4,128)S(1)}, s32[4,768]{1,0:T(4,128)}, u32[]{:S(2)}) copy-start(s32[4,768]{1,0:T(4,128)} %param.4) | copy-start | bytes 36868
  3.1 6.5 %copy-start = (s32[6,3]{0,1:T(4,128)S(1)}, s32[6,3]{0,1:T(4,128)}, u32[]{:S(2)}) copy-start(s32[6,3]{0,1:T(4,128)} %param.7) | copy-start | bytes 220
  7.0 7.2 %collective-permute-start.1 = (s32[8,768]{1,0:T(8,128)S(1)}, s32[8,768]{1,0:T(8,128)S(1)}, u32[]{:S(2)}, u32[]{:S(2)}) collective-permute-start(s32[8,768]{1,0:T(8,128)S(1)} %pad_add_fusion.1), channel_id=1, source_target_pairs={{8,0},{12,4},{0,8},{4,12},{9,1},{13,5},{1,9},{5,13},{10,2},{14,6},... | collective-permute-start | bytes 73736 | tf_op jit(solution)/shard_map/ppermute | solution.py:289
  22.0 12.5 %collective-permute-start.2 = (f32[128,768]{1,0:T(8,128)S(1)}, f32[128,768]{1,0:T(8,128)S(1)}, u32[]{:S(2)}, u32[]{:S(2)}) collective-permute-start(f32[128,768]{1,0:T(8,128)S(1)} %get-tuple-element.16.mine_ref), channel_id=1, source_target_pairs={{0,1},{1,0},{2,3},{3,2},{4,5},{5,4},{6,7},{7,6},{8,9},{9,8},{10,11... | collective-permute-start | bytes 1179656 | tf_op jit(solution)/shard_map/ppermute | solution.py:358
  40.9 2.9 %collective-permute-start.3 = (f32[384,768]{1,0:T(8,128)S(1)}, f32[384,768]{1,0:T(8,128)S(1)}, u32[]{:S(2)}, u32[]{:S(2)}) collective-permute-start(f32[384,768]{1,0:T(8,128)S(1)} %get-tuple-element.19.rows_ref), channel_id=1, source_target_pairs={{0,2},{2,0},{1,3},{3,1},{4,6},{6,4},{5,7},{7,5},{8,10},{10,8},{9,1... | collective-permute-start | bytes 3538952 | tf_op jit(solution)/shard_map/ppermute | solution.py:372

commit v6 on v5

--- a/solution.py
+++ b/solution.py
@@ -15,6 +15,10 @@
 
 def dot(left, right):
     return jnp.dot(left, right, preferred_element_type=F32)
+
+
+def dot_by(left, right, width):
+    return jnp.concatenate([dot(left, right[:, at : at + width]) for at in range(0, right.shape[1], width)], axis=1)
 
 
 def split(x):
@@ -181,15 +185,15 @@
         lax.fori_loop(peeled, steps, lambda step, carry: (one_slice(steps - 1 - step, n_tiles), carry)[1], 0)
 
 
-def corrected(places, tile_len, p_high_ref, p_low_ref, guess_ref):
+def corrected(places, tile_len, excess_ref, p_high_ref, p_low_ref, guess_ref):
     def rows_of(ref):
         return jnp.concatenate([ref[tile_ds(p, tile_len), :] for p in places], axis=0)
 
     guess = rows_of(guess_ref)
-    guess32 = guess.astype(F32)
-    p_rows = rows_of(p_high_ref).astype(F32) + rows_of(p_low_ref).astype(F32)
-    residual = (guess32 - p_rows) + (dot(guess, p_high_ref[...]) + dot(guess, p_low_ref[...]))
-    return guess32 - residual + dot(residual.astype(BF16), guess_ref[...])
+    guess8 = (guess.astype(F32) * 2.0**8).astype(F8)
+    small = dot_by(guess8, p_low_ref[...], 2 * tile_len) * 2.0**-25
+    residual = rows_of(excess_ref) + dot_by(guess, p_high_ref[...], 2 * tile_len) + small
+    return (guess.astype(F32) - residual) + dot_by(residual.astype(BF16), guess_ref[...], 2 * tile_len)
 
 
 def tiles_of_rows(where_ref, n_tiles, own_tiles):
@@ -216,7 +220,7 @@
 
 def green_kernel(
     n_tiles, tile_len, own_tiles, tile_cols_ref, where_ref, mine_ref, theirs_ref, common_ref, last_ref,
-    rows_ref, guess_ref, p_high_ref, p_low_ref, b_ref, c_ref, one8_ref, two8_ref, part8_ref, four8_ref,
+    rows_ref, excess_ref, guess_ref, p_high_ref, p_low_ref, p_ref, c_ref, one8_ref, two8_ref, part8_ref, four8_ref,
 ):
     order = cycle_order(tile_cols_ref, n_tiles)
     matrix_order = mine_ref.shape[1]
@@ -231,34 +235,38 @@
     shrink = 0.5 / jnp.max(col_sum, axis=1, keepdims=True)
     for p, piece in enumerate(pieces):
         rows = slice(p * tile_len, (p + 1) * tile_len)
-        p_rows = piece * shrink
-        p_high_ref[rows, :], p_low_ref[rows, :] = split(p_rows)
+        p_ref[rows, :] = piece * shrink
+        p_high_ref[rows, :] = p_ref[rows, :].astype(BF16)
+    for rows in blocks:
+        square = dot_by(p_high_ref[rows, :], p_high_ref[...], block)
+        two8_ref[rows, :] = (square * 2.0**10).astype(F8)
+        p_rows = p_ref[rows, :]
+        p_low_ref[rows, :] = ((p_rows - p_high_ref[rows, :].astype(F32)) * 2.0**17).astype(F8)
         one8_ref[rows, :] = (p_rows * 2.0**9).astype(F8)
-    for rows in blocks:
-        square = dot(p_high_ref[rows, :], p_high_ref[...])
-        b_ref[rows, :] = square.astype(BF16)
-        two8_ref[rows, :] = (square * 2.0**10).astype(F8)
+        c_ref[rows, :] = square - p_rows
     for rows in blocks:
         square = two8_ref[rows, :]
-        cube = dot(square, one8_ref[...]) * 2.0**-19
-        part = b_ref[rows, :].astype(F32) - p_high_ref[rows, :].astype(F32) - cube
-        fourth = dot(square, two8_ref[...]) * 2.0**-20
+        cube = dot_by(square, one8_ref[...], block) * 2.0**-19
+        part = c_ref[rows, :] - cube
+        fourth = dot_by(square, two8_ref[...], block) * 2.0**-20
         c_ref[rows, :] = part + fourth
         part8_ref[rows, :] = (part * 2.0**8).astype(F8)
         four8_ref[rows, :] = (fourth * 2.0**12).astype(F8)
     for rows in blocks:
-        guess_ref[rows, :] = (-(c_ref[rows, :] + dot(part8_ref[rows, :], four8_ref[...]) * 2.0**-20)).astype(BF16)
+        guess = (-(c_ref[rows, :] + dot_by(part8_ref[rows, :], four8_ref[...], block) * 2.0**-20)).astype(BF16)
+        guess_ref[rows, :] = guess
+        excess_ref[rows, :] = guess.astype(F32) - p_ref[rows, :]
 
     own, _ = tiles_of_rows(where_ref, n_tiles, own_tiles)
-    y = corrected([place_of(order, t) for t in own], tile_len, p_high_ref, p_low_ref, guess_ref)
+    y = corrected([place_of(order, t) for t in own], tile_len, excess_ref, p_high_ref, p_low_ref, guess_ref)
     for q in range(n_tiles):
         rows_ref[:, tile_ds(order[q], tile_len)] = y[:, q * tile_len : (q + 1) * tile_len]
 
 
-def rest_kernel(n_tiles, tile_len, own_tiles, tile_cols_ref, where_ref, guess_ref, p_high_ref, p_low_ref, out_ref, y_ref):
+def rest_kernel(n_tiles, tile_len, own_tiles, tile_cols_ref, where_ref, excess_ref, guess_ref, p_high_ref, p_low_ref, out_ref, y_ref):
     order = cycle_order(tile_cols_ref, n_tiles)
     own, rest = tiles_of_rows(where_ref, n_tiles, own_tiles)
-    y_ref[...] = corrected([place_of(order, t) for t in rest], tile_len, p_high_ref, p_low_ref, guess_ref)
+    y_ref[...] = corrected([place_of(order, t) for t in rest], tile_len, excess_ref, p_high_ref, p_low_ref, guess_ref)
     for i, t in enumerate(own):
         out_ref[:, i * tile_len : (i + 1) * tile_len] = y_ref[:, tile_ds(place_of(order, t), tile_len)]
 
@@ -357,12 +365,13 @@
     mine, common = chain_part(ahead, [mine, common], shared_tile, common_tiles)
     theirs = lax.ppermute(mine, "rows", [(i, i ^ 1) for i in range(n_rows)])
     (last,) = chain_part(ahead, [last], last_tiles)
-    rows, guess, p_high, p_low = pl.pallas_call(
+    rows, excess, guess, p_high, p_low = pl.pallas_call(
         functools.partial(green_kernel, *sizes),
-        out_shape=[jax.ShapeDtypeStruct((own_len, matrix_order), F32)] + [jax.ShapeDtypeStruct(square, BF16)] * 3,
+        out_shape=[jax.ShapeDtypeStruct((own_len, matrix_order), F32), jax.ShapeDtypeStruct(square, F32)]
+        + [jax.ShapeDtypeStruct(square, dtype) for dtype in (BF16, BF16, F8)],
         in_specs=[smem, smem] + [vmem] * 4,
-        out_specs=[vmem] * 4,
-        scratch_shapes=[pltpu.VMEM(square, BF16), pltpu.VMEM(square, F32)]
+        out_specs=[vmem] * 5,
+        scratch_shapes=[pltpu.VMEM(square, F32)] * 2
         + [pltpu.VMEM(square, F8)] * 4,
         compiler_params=pltpu.CompilerParams(vmem_limit_bytes=32 * 2**20),
         cost_estimate=pl.CostEstimate(flops=5 * 10**9, bytes_accessed=6 * 10**6, transcendentals=0),
@@ -373,13 +382,13 @@
     rest = pl.pallas_call(
         functools.partial(rest_kernel, *sizes),
         out_shape=jax.ShapeDtypeStruct((matrix_order - own_len, own_len), F32),
-        in_specs=[smem, smem, vmem, vmem, vmem],
+        in_specs=[smem, smem, vmem, vmem, vmem, vmem],
         out_specs=vmem,
         scratch_shapes=[pltpu.VMEM((matrix_order - own_len, matrix_order), F32)],
         compiler_params=pltpu.CompilerParams(vmem_limit_bytes=24 * 2**20),
         cost_estimate=pl.CostEstimate(flops=2 * 10**9, bytes_accessed=4 * 10**6, transcendentals=0),
         name="rest",
-    )(cols_of_tiles, where, guess, p_high, p_low)
+    )(cols_of_tiles, where, excess, guess, p_high, p_low)
     xcorr = pl.pallas_call(
         functools.partial(xcorr_kernel, *sizes),
         out_shape=jax.ShapeDtypeStruct((matrix_order, own_len), F32),

time: 45.9 us -> 45.6 us (level)
  Pallas kernels: 37.6 us -> 36.9 us
where the time goes in v6:
time: 45.6 us; the launch traced here: 45.4 us
  Pallas kernels  36.9 us (81%)
  starting transfers between devices  7.25 us (16%)
  waiting for transfers between devices  0.86 us (2%)
    pallas_call x3, Pallas kernels, chain_part(): pl.pallas_call(functools.partial(chain_kernel, n_tiles, tile_len, couplin...  23.3 us
    pallas_call x1, Pallas kernels, per_device(): pl.pallas_call(functools.partial(green_kernel, *sizes), out_shape=[jax.Sh...  6.04 us
    ppermute x2, starting transfers between devices, from_ahead(): return lax.ppermute(x, axis, [((i + by) % size, i) for i in range(size)])  5.63 us
    pallas_call x1, Pallas kernels, per_device(): pl.pallas_call(functools.partial(kinetic_kernel, n_tiles, tile_len, 0.5 /...  3.74 us
    pallas_call x1, Pallas kernels, per_device(): pl.pallas_call(functools.partial(rest_kernel, *sizes), out_shape=jax.Shap...  2.05 us
    pallas_call x1, Pallas kernels, per_device(): pl.pallas_call(functools.partial(xcorr_kernel, *sizes), out_shape=jax.Sha...  1.73 us
    ppermute x1, starting transfers between devices, per_device(): theirs = lax.ppermute(mine, 'rows', [(i, i ^ 1) for i in range(n_rows)])  1.55 us
  transfers between devices with their start and end apart: 4, of which 2 were waited for; matrix products, arithmetic and copies ran while one was open for 0% of the time, Pallas kernels for 47%

profile of v6, /device:TPU:0, one launch (start us, length us, event | category | flops | bytes accessed | tf_op | source)
XLA Modules:
  0.0 45.4 jit_solution(5425829038501188890)
XLA Ops:
  0.0 3.1 %collective-permute-start = (s32[4,768]{1,0:T(4,128)}, s32[4,768]{1,0:T(4,128)S(1)}, u32[]{:S(2)}, u32[]{:S(2)}) collective-permute-start(s32[4,768]{1,0:T(4,128)} %param.4), channel_id=1, source_target_pairs={{12,0},{0,4},{4,8},{8,12},{13,1},{1,5},{5,9},{9,13},{14,2},{2,6},{... | collective-permute-start | bytes 36872 | tf_op jit(solution)/shard_map/ppermute | solution.py:297
  3.1 0.0 copy-start.1
  3.1 0.0 copy-start
  3.1 3.7 %kinetic.1.weight_ref = bf16[3,1024,256]{2,1,0:T(8,128)(2,1)S(1)} custom-call(s32[3,6]{1,0:T(4,128)} %bitcast.7, s32[2,3072]{1,0:T(2,128)} %bitcast.13, f32[1,3072]{1,0:T(1,128)} %bitcast.14), custom_call_target="tpu_custom_call" | custom-call | flops 4000000000 | bytes 4000000 | tf_op jit(solution)/shard_map/kinetic/pallas_call | solution.py:329
  6.8 0.1 pad_add_fusion.2.where_ref
  6.9 0.1 collective-permute-done.field_ref
  7.0 0.0 copy-done.1
  7.0 2.6 %collective-permute-start.1 = (s32[8,768]{1,0:T(8,128)S(1)}, s32[8,768]{1,0:T(8,128)S(1)}, u32[]{:S(2)}, u32[]{:S(2)}) collective-permute-start(s32[8,768]{1,0:T(8,128)S(1)} %pad_add_fusion.1), channel_id=1, source_target_pairs={{8,0},{12,4},{0,8},{4,12},{9,1},{13,5},{1,9},{5,13},{10,2},{14,6},... | collective-permute-start | bytes 73736 | tf_op jit(solution)/shard_map/ppermute | solution.py:297
  9.6 0.0 copy-done
  9.6 4.6 %chain.3 = (f32[128,768]{1,0:T(8,128)S(1)}, f32[128,768]{1,0:T(8,128)S(1)}, f32[384,768]{1,0:T(8,128)S(1)}) custom-call(s32[3,6]{1,0:T(4,128)S(1)} %bitcast.8, s32[3]{0:T(128)S(1)} %pad_add_fusion.2.where_ref, s32[4,768]{1,0:T(4,128)S(1)} %collective-permute-done.field_ref, bf16[3,1024,256]{2,1,0:T(8,128)(2,1)S(1)} %kinetic.1.weight_ref), custom_call_target="tpu_custom_call" | custom-call | flops 6400000000 | bytes 4000000 | tf_op jit(solution)/shard_map/chain/pallas_call | solution.py:351
  14.1 0.0 collective-permute-done.1
  14.2 7.8 %chain.4 = (f32[128,768]{1,0:T(8,128)S(1)}, f32[128,768]{1,0:T(8,128)S(1)}) custom-call(s32[3,6]{1,0:T(4,128)S(1)} %bitcast.9, s32[3]{0:T(128)S(1)} %pad_add_fusion.2.where_ref, s32[12,768]{1,0:T(8,128)S(1)} %pad_add_fusion.field_ref, bf16[3,1024,256]{2,1,0:T(8,128)(2,1)S(1)} %kinetic.1.weight_ref, f32[128,768]{1,0:T(8,128)S(1)} %get-tuple-element.15.refs_0_, ...), custom_call_target="tpu_custom_call" | custom-call | flops 7680000000 | bytes 4000000 | tf_op jit(solution)/shard_map/chain/pallas_call | solution.py:351
  22.0 1.5 %collective-permute-start.2 = (f32[128,768]{1,0:T(8,128)S(1)}, f32[128,768]{1,0:T(8,128)S(1)}, u32[]{:S(2)}, u32[]{:S(2)}) collective-permute-start(f32[128,768]{1,0:T(8,128)S(1)} %get-tuple-element.17.mine_ref), channel_id=1, source_target_pairs={{0,1},{1,0},{2,3},{3,2},{4,5},{5,4},{6,7},{7,6},{8,9},{9,8},{10,11... | collective-permute-start | bytes 1179656 | tf_op jit(solution)/shard_map/ppermute | solution.py:366
  23.6 10.9 %chain.5.last_ref = f32[384,768]{1,0:T(8,128)S(1)} custom-call(s32[3,6]{1,0:T(4,128)S(1)} %bitcast.10, s32[3]{0:T(128)S(1)} %pad_add_fusion.2.where_ref, s32[12,768]{1,0:T(8,128)S(1)} %pad_add_fusion.field_ref, bf16[3,1024,256]{2,1,0:T(8,128)(2,1)S(1)} %kinetic.1.weight_ref, f32[384,768]{1,0:T(8,128)S(1)} %get-tuple-element.19.refs_0_), custom_call_target="tpu_custom_call" | custom-call | flops 11520000000 | bytes 4000000 | tf_op jit(solution)/shard_map/chain/pallas_call | solution.py:351
  34.5 0.0 collective-permute-done.2.theirs_ref
  34.5 6.0 %green.1 = (f32[384,768]{1,0:T(8,128)S(1)}, f32[768,768]{1,0:T(8,128)S(1)}, bf16[768,768]{1,0:T(8,128)(2,1)S(1)}, bf16[768,768]{1,0:T(8,128)(2,1)S(1)}, f8e4m3fn[768,768]{1,0:T(32,128)(4,1)S(1)}) custom-call(s32[3,6]{1,0:T(4,128)S(1)} %bitcast.11, s32[3]{0:T(128)S(1)} %pad_add_fusion.2.where_ref, f32[128,768]{1,0:T(8,128)S(1)} %get-tuple-element.17.mine_ref, ...), custom_call_target="tpu_custom_call" | custom-call | flops 5000000000 | bytes 6000000 | tf_op jit(solution)/shard_map/green/pallas_call | solution.py:368
  40.6 0.1 collective-permute-start.3
  40.6 2.1 %rest.1.rest_ref = f32[384,384]{1,0:T(8,128)S(1)} custom-call(s32[3,6]{1,0:T(4,128)S(1)} %bitcast.12, s32[3]{0:T(128)S(1)} %pad_add_fusion.2.where_ref, f32[768,768]{1,0:T(8,128)S(1)} %get-tuple-element.21.excess_ref, bf16[768,768]{1,0:T(8,128)(2,1)S(1)} %get-tuple-element.22.guess_ref, bf16[768,768]{1,0:T(8,128)(2,1)S(1)} %get-tuple-element.23.p_high_ref, ...), custom_call_target="tpu_custom_call" | custom-call | flops 2000000000 | bytes 4000000 | tf_op jit(solution)/shard_map/rest/pallas_call | solution.py:382
  42.7 0.8 %collective-permute-done.3.other_ref = f32[384,768]{1,0:T(8,128)S(1)} collective-permute-done((f32[384,768]{1,0:T(8,128)S(1)}, f32[384,768]{1,0:T(8,128)S(1)}, u32[]{:S(2)}, u32[]{:S(2)}) %collective-permute-start.3) | collective-permute-done | bytes 1179680 | tf_op jit(solution)/shard_map/ppermute | solution.py:381
  43.5 1.7 %xcorr.1 = f32[768,384]{1,0:T(8,128)} custom-call(s32[3]{0:T(128)S(1)} %pad_add_fusion.2.where_ref, f32[384,768]{1,0:T(8,128)S(1)} %get-tuple-element.20.rows_ref, f32[384,384]{1,0:T(8,128)S(1)} %rest.1.rest_ref, f32[384,768]{1,0:T(8,128)S(1)} %collective-permute-done.3.other_ref), custom_call_target="tpu_custom_call" | custom-call | tf_op jit(solution)/shard_map/xcorr/pallas_call | solution.py:392
  (2 shorter events, 0.0 us)
Async XLA Ops:
  0.0 7.0 %collective-permute-start = (s32[4,768]{1,0:T(4,128)}, s32[4,768]{1,0:T(4,128)S(1)}, u32[]{:S(2)}, u32[]{:S(2)}) collective-permute-start(s32[4,768]{1,0:T(4,128)} %param.4), channel_id=1, source_target_pairs={{12,0},{0,4},{4,8},{8,12},{13,1},{1,5},{5,9},{9,13},{14,2},{2,6},{... | collective-permute-start | bytes 36872 | tf_op jit(solution)/shard_map/ppermute | solution.py:297
  3.1 3.9 %copy-start.1 = (s32[4,768]{1,0:T(4,128)S(1)}, s32[4,768]{1,0:T(4,128)}, u32[]{:S(2)}) copy-start(s32[4,768]{1,0:T(4,128)} %param.4) | copy-start | bytes 36868
  3.1 6.5 %copy-start = (s32[6,3]{0,1:T(4,128)S(1)}, s32[6,3]{0,1:T(4,128)}, u32[]{:S(2)}) copy-start(s32[6,3]{0,1:T(4,128)} %param.7) | copy-start | bytes 220
  7.0 7.2 %collective-permute-start.1 = (s32[8,768]{1,0:T(8,128)S(1)}, s32[8,768]{1,0:T(8,128)S(1)}, u32[]{:S(2)}, u32[]{:S(2)}) collective-permute-start(s32[8,768]{1,0:T(8,128)S(1)} %pad_add_fusion.1), channel_id=1, source_target_pairs={{8,0},{12,4},{0,8},{4,12},{9,1},{13,5},{1,9},{5,13},{10,2},{14,6},... | collective-permute-start | bytes 73736 | tf_op jit(solution)/shard_map/ppermute | solution.py:297
  22.0 12.5 %collective-permute-start.2 = (f32[128,768]{1,0:T(8,128)S(1)}, f32[128,768]{1,0:T(8,128)S(1)}, u32[]{:S(2)}, u32[]{:S(2)}) collective-permute-start(f32[128,768]{1,0:T(8,128)S(1)} %get-tuple-element.17.mine_ref), channel_id=1, source_target_pairs={{0,1},{1,0},{2,3},{3,2},{4,5},{5,4},{6,7},{7,6},{8,9},{9,8},{10,11... | collective-permute-start | bytes 1179656 | tf_op jit(solution)/shard_map/ppermute | solution.py:366
  40.6 2.9 %collective-permute-start.3 = (f32[384,768]{1,0:T(8,128)S(1)}, f32[384,768]{1,0:T(8,128)S(1)}, u32[]{:S(2)}, u32[]{:S(2)}) collective-permute-start(f32[384,768]{1,0:T(8,128)S(1)} %get-tuple-element.20.rows_ref), channel_id=1, source_target_pairs={{0,2},{2,0},{1,3},{3,1},{4,6},{6,4},{5,7},{7,5},{8,10},{10,8},{9,1... | collective-permute-start | bytes 3538952 | tf_op jit(solution)/shard_map/ppermute | solution.py:381

commit v7 on v6

--- a/solution.py
+++ b/solution.py
@@ -62,7 +62,7 @@
     shift = tile_len.bit_length() - 1
     bonds = sites_ref.shape[1]
     pair_len = 2 * tile_len
-    chunk = min(bonds, 512)
+    chunk = min(bonds, 1024)
 
     def position(site):
         tile = site >> shift

time: 45.6 us -> 45.6 us (level)
  transfers between devices with their start and end apart: 4 -> 4, of which waited for: 2 -> 1; matrix products, arithmetic and copies ran while one was open for 0% -> 0% of each run, Pallas kernels for 47% -> 47%
where the time goes in v7:
time: 45.6 us; the launch traced here: 45.5 us
  Pallas kernels  37 us (81%)
  starting transfers between devices  7.3 us (16%)
  waiting for transfers between devices  0.82 us (2%)
    pallas_call x3, Pallas kernels, chain_part(): pl.pallas_call(functools.partial(chain_kernel, n_tiles, tile_len, couplin...  23.3 us
    pallas_call x1, Pallas kernels, per_device(): pl.pallas_call(functools.partial(green_kernel, *sizes), out_shape=[jax.Sh...  6.05 us
    ppermute x2, starting transfers between devices, from_ahead(): return lax.ppermute(x, axis, [((i + by) % size, i) for i in range(size)])  5.68 us
    pallas_call x1, Pallas kernels, per_device(): pl.pallas_call(functools.partial(kinetic_kernel, n_tiles, tile_len, 0.5 /...  3.78 us
    pallas_call x1, Pallas kernels, per_device(): pl.pallas_call(functools.partial(rest_kernel, *sizes), out_shape=jax.Shap...  2.05 us
    pallas_call x1, Pallas kernels, per_device(): pl.pallas_call(functools.partial(xcorr_kernel, *sizes), out_shape=jax.Sha...  1.73 us
    ppermute x1, starting transfers between devices, per_device(): theirs = lax.ppermute(mine, 'rows', [(i, i ^ 1) for i in range(n_rows)])  1.55 us
  transfers between devices with their start and end apart: 4, of which 1 were waited for; matrix products, arithmetic and copies ran while one was open for 0% of the time, Pallas kernels for 47%

profile of v7, /device:TPU:0, one launch (start us, length us, event | category | flops | bytes accessed | tf_op | source)
XLA Modules:
  0.0 45.5 jit_solution(7707241787394797794)
XLA Ops:
  0.0 3.1 %collective-permute-start = (s32[4,768]{1,0:T(4,128)}, s32[4,768]{1,0:T(4,128)S(1)}, u32[]{:S(2)}, u32[]{:S(2)}) collective-permute-start(s32[4,768]{1,0:T(4,128)} %param.4), channel_id=1, source_target_pairs={{12,0},{0,4},{4,8},{8,12},{13,1},{1,5},{5,9},{9,13},{14,2},{2,6},{... | collective-permute-start | bytes 36872 | tf_op jit(solution)/shard_map/ppermute | solution.py:297
  3.1 0.0 copy-start.1
  3.1 0.0 copy-start
  3.1 3.8 %kinetic.1.weight_ref = bf16[3,1024,256]{2,1,0:T(8,128)(2,1)S(1)} custom-call(s32[3,6]{1,0:T(4,128)} %bitcast.7, s32[2,3072]{1,0:T(2,128)} %bitcast.13, f32[1,3072]{1,0:T(1,128)} %bitcast.14), custom_call_target="tpu_custom_call" | custom-call | flops 4000000000 | bytes 4000000 | tf_op jit(solution)/shard_map/kinetic/pallas_call | solution.py:329
  6.8 0.1 pad_add_fusion.2.where_ref
  6.9 0.0 collective-permute-done.field_ref
  7.0 0.0 copy-done.1
  7.0 2.6 %collective-permute-start.1 = (s32[8,768]{1,0:T(8,128)S(1)}, s32[8,768]{1,0:T(8,128)S(1)}, u32[]{:S(2)}, u32[]{:S(2)}) collective-permute-start(s32[8,768]{1,0:T(8,128)S(1)} %pad_add_fusion.1), channel_id=1, source_target_pairs={{8,0},{12,4},{0,8},{4,12},{9,1},{13,5},{1,9},{5,13},{10,2},{14,6},... | collective-permute-start | bytes 73736 | tf_op jit(solution)/shard_map/ppermute | solution.py:297
  9.6 0.0 copy-done
  9.6 4.6 %chain.3 = (f32[128,768]{1,0:T(8,128)S(1)}, f32[128,768]{1,0:T(8,128)S(1)}, f32[384,768]{1,0:T(8,128)S(1)}) custom-call(s32[3,6]{1,0:T(4,128)S(1)} %bitcast.8, s32[3]{0:T(128)S(1)} %pad_add_fusion.2.where_ref, s32[4,768]{1,0:T(4,128)S(1)} %collective-permute-done.field_ref, bf16[3,1024,256]{2,1,0:T(8,128)(2,1)S(1)} %kinetic.1.weight_ref), custom_call_target="tpu_custom_call" | custom-call | flops 6400000000 | bytes 4000000 | tf_op jit(solution)/shard_map/chain/pallas_call | solution.py:351
  14.2 0.0 collective-permute-done.1
  14.2 7.8 %chain.4 = (f32[128,768]{1,0:T(8,128)S(1)}, f32[128,768]{1,0:T(8,128)S(1)}) custom-call(s32[3,6]{1,0:T(4,128)S(1)} %bitcast.9, s32[3]{0:T(128)S(1)} %pad_add_fusion.2.where_ref, s32[12,768]{1,0:T(8,128)S(1)} %pad_add_fusion.field_ref, bf16[3,1024,256]{2,1,0:T(8,128)(2,1)S(1)} %kinetic.1.weight_ref, f32[128,768]{1,0:T(8,128)S(1)} %get-tuple-element.15.refs_0_, ...), custom_call_target="tpu_custom_call" | custom-call | flops 7680000000 | bytes 4000000 | tf_op jit(solution)/shard_map/chain/pallas_call | solution.py:351
  22.1 1.6 %collective-permute-start.2 = (f32[128,768]{1,0:T(8,128)S(1)}, f32[128,768]{1,0:T(8,128)S(1)}, u32[]{:S(2)}, u32[]{:S(2)}) collective-permute-start(f32[128,768]{1,0:T(8,128)S(1)} %get-tuple-element.17.mine_ref), channel_id=1, source_target_pairs={{0,1},{1,0},{2,3},{3,2},{4,5},{5,4},{6,7},{7,6},{8,9},{9,8},{10,11... | collective-permute-start | bytes 1179656 | tf_op jit(solution)/shard_map/ppermute | solution.py:366
  23.6 10.9 %chain.5.last_ref = f32[384,768]{1,0:T(8,128)S(1)} custom-call(s32[3,6]{1,0:T(4,128)S(1)} %bitcast.10, s32[3]{0:T(128)S(1)} %pad_add_fusion.2.where_ref, s32[12,768]{1,0:T(8,128)S(1)} %pad_add_fusion.field_ref, bf16[3,1024,256]{2,1,0:T(8,128)(2,1)S(1)} %kinetic.1.weight_ref, f32[384,768]{1,0:T(8,128)S(1)} %get-tuple-element.19.refs_0_), custom_call_target="tpu_custom_call" | custom-call | flops 11520000000 | bytes 4000000 | tf_op jit(solution)/shard_map/chain/pallas_call | solution.py:351
  34.6 0.0 collective-permute-done.2.theirs_ref
  34.6 6.0 %green.1 = (f32[384,768]{1,0:T(8,128)S(1)}, f32[768,768]{1,0:T(8,128)S(1)}, bf16[768,768]{1,0:T(8,128)(2,1)S(1)}, bf16[768,768]{1,0:T(8,128)(2,1)S(1)}, f8e4m3fn[768,768]{1,0:T(32,128)(4,1)S(1)}) custom-call(s32[3,6]{1,0:T(4,128)S(1)} %bitcast.11, s32[3]{0:T(128)S(1)} %pad_add_fusion.2.where_ref, f32[128,768]{1,0:T(8,128)S(1)} %get-tuple-element.17.mine_ref, ...), custom_call_target="tpu_custom_call" | custom-call | flops 5000000000 | bytes 6000000 | tf_op jit(solution)/shard_map/green/pallas_call | solution.py:368
  40.6 0.1 collective-permute-start.3
  40.7 2.0 %rest.1.rest_ref = f32[384,384]{1,0:T(8,128)S(1)} custom-call(s32[3,6]{1,0:T(4,128)S(1)} %bitcast.12, s32[3]{0:T(128)S(1)} %pad_add_fusion.2.where_ref, f32[768,768]{1,0:T(8,128)S(1)} %get-tuple-element.21.excess_ref, bf16[768,768]{1,0:T(8,128)(2,1)S(1)} %get-tuple-element.22.guess_ref, bf16[768,768]{1,0:T(8,128)(2,1)S(1)} %get-tuple-element.23.p_high_ref, ...), custom_call_target="tpu_custom_call" | custom-call | flops 2000000000 | bytes 4000000 | tf_op jit(solution)/shard_map/rest/pallas_call | solution.py:382
  42.8 0.8 %collective-permute-done.3.other_ref = f32[384,768]{1,0:T(8,128)S(1)} collective-permute-done((f32[384,768]{1,0:T(8,128)S(1)}, f32[384,768]{1,0:T(8,128)S(1)}, u32[]{:S(2)}, u32[]{:S(2)}) %collective-permute-start.3) | collective-permute-done | bytes 1179680 | tf_op jit(solution)/shard_map/ppermute | solution.py:381
  43.5 1.7 %xcorr.1 = f32[768,384]{1,0:T(8,128)} custom-call(s32[3]{0:T(128)S(1)} %pad_add_fusion.2.where_ref, f32[384,768]{1,0:T(8,128)S(1)} %get-tuple-element.20.rows_ref, f32[384,384]{1,0:T(8,128)S(1)} %rest.1.rest_ref, f32[384,768]{1,0:T(8,128)S(1)} %collective-permute-done.3.other_ref), custom_call_target="tpu_custom_call" | custom-call | tf_op jit(solution)/shard_map/xcorr/pallas_call | solution.py:392
  (2 shorter events, 0.0 us)
Async XLA Ops:
  0.0 7.0 %collective-permute-start = (s32[4,768]{1,0:T(4,128)}, s32[4,768]{1,0:T(4,128)S(1)}, u32[]{:S(2)}, u32[]{:S(2)}) collective-permute-start(s32[4,768]{1,0:T(4,128)} %param.4), channel_id=1, source_target_pairs={{12,0},{0,4},{4,8},{8,12},{13,1},{1,5},{5,9},{9,13},{14,2},{2,6},{... | collective-permute-start | bytes 36872 | tf_op jit(solution)/shard_map/ppermute | solution.py:297
  3.1 3.9 %copy-start.1 = (s32[4,768]{1,0:T(4,128)S(1)}, s32[4,768]{1,0:T(4,128)}, u32[]{:S(2)}) copy-start(s32[4,768]{1,0:T(4,128)} %param.4) | copy-start | bytes 36868
  3.1 6.6 %copy-start = (s32[6,3]{0,1:T(4,128)S(1)}, s32[6,3]{0,1:T(4,128)}, u32[]{:S(2)}) copy-start(s32[6,3]{0,1:T(4,128)} %param.7) | copy-start | bytes 220
  7.0 7.2 %collective-permute-start.1 = (s32[8,768]{1,0:T(8,128)S(1)}, s32[8,768]{1,0:T(8,128)S(1)}, u32[]{:S(2)}, u32[]{:S(2)}) collective-permute-start(s32[8,768]{1,0:T(8,128)S(1)} %pad_add_fusion.1), channel_id=1, source_target_pairs={{8,0},{12,4},{0,8},{4,12},{9,1},{13,5},{1,9},{5,13},{10,2},{14,6},... | collective-permute-start | bytes 73736 | tf_op jit(solution)/shard_map/ppermute | solution.py:297
  22.1 12.5 %collective-permute-start.2 = (f32[128,768]{1,0:T(8,128)S(1)}, f32[128,768]{1,0:T(8,128)S(1)}, u32[]{:S(2)}, u32[]{:S(2)}) collective-permute-start(f32[128,768]{1,0:T(8,128)S(1)} %get-tuple-element.17.mine_ref), channel_id=1, source_target_pairs={{0,1},{1,0},{2,3},{3,2},{4,5},{5,4},{6,7},{7,6},{8,9},{9,8},{10,11... | collective-permute-start | bytes 1179656 | tf_op jit(solution)/shard_map/ppermute | solution.py:366
  40.6 2.9 %collective-permute-start.3 = (f32[384,768]{1,0:T(8,128)S(1)}, f32[384,768]{1,0:T(8,128)S(1)}, u32[]{:S(2)}, u32[]{:S(2)}) collective-permute-start(f32[384,768]{1,0:T(8,128)S(1)} %get-tuple-element.20.rows_ref), channel_id=1, source_target_pairs={{0,2},{2,0},{1,3},{3,1},{4,6},{6,4},{5,7},{7,5},{8,10},{10,8},{9,1... | collective-permute-start | bytes 3538952 | tf_op jit(solution)/shard_map/ppermute | solution.py:381
